TPU v7x, 32 devices: a whole 2x2x4 slice. The times are simulated.
32 devices in a mesh: grp: 4 (over x, core), dom: 8 (over z, y).
Axes of the slice: x: 2, y: 2, z: 4, core: 2. Of those that a mesh axis runs over, the one named last changes fastest.
Arguments:
- cell_index: int32 [3, 65536], P(None, ('grp', 'dom')), may hold values from 0 to 255, as said below
- offsets: float32 [3, 65536], P(None, ('grp', 'dom')), may hold values from -0.5 to 0.5
- species: int32 [65536], P(('grp', 'dom')), may hold values from 0 to 7
- pair_blocks: int32 [128, 2], P(('grp', 'dom')), may hold values from 0 to 47, as said below
- counts: int32 [32], P(('grp', 'dom')), may hold values from 1 to 4, as said below
- background: float32 [256, 256, 256], P('dom', 'grp'), may hold values from -0.12 to 0.12
- species_embed: float32 [8, 256], replicated, may hold values from -6 to 6
- neighbour_embed: float32 [8, 256], replicated, may hold values from -6 to 6
- w_radial: float32 [8, 256], replicated, may hold values from -2 to 2
- w_hidden: bfloat16 [256, 256], replicated, may hold values from -0.375 to 0.375
- w_charge: bfloat16 [256], replicated, may hold values from -0.375 to 0.375
- w_energy: bfloat16 [256], replicated, may hold values from -0.375 to 0.375
Outputs:
- site_energy: float32 [65536], P(('grp', 'dom'))
- electric_field: float32 [3, 65536], P(None, ('grp', 'dom'))
- charges: float32 [65536], P(('grp', 'dom'))
Inputs may be any that keep to these rules, and one draw needn't show every extreme that they name: `cell_index`: atoms of domain k = g * 8 + d (atoms k * 2048 on) have a first index in [32 d, 32 d + 32) and a second in [64 g, 64 g + 64). Atom block b of a domain lies in second-index tile b mod 4 of width 64 / 4 and third-index tile b // 4 of width 256 / 4. `pair_blocks`: the i block is one of the domain's 16 blocks; the j block indexes the 48 extended blocks and lies in the same or an adjacent tile of its domain. `counts`: some device has exactly 4 live slots in every draw.
All inputs are finite; a program needn't handle non-finite values.
Results may differ from a plain program's by a relative error of at most 0.0003.
The roundings to bfloat16 on the way count: a program that leaves them out, or rounds other values in their place, can miss the bound.
Values sent between devices are 32-bit elements; how exact they have to be, the bound alone decides.
A program may use at most 128 MiB of HBM per device.

v0:
```python
import math

import jax
import jax.numpy as jnp
from jax import lax
from jax.sharding import PartitionSpec as P

G = 256
NBASIS = 8
NSPEC = 8
BLOCK = 128


CUTOFF = 6.0
EWALD = 1.0
HIGHEST = lax.Precision.HIGHEST


def padded(cells, sides, width):
    for axis, dim in sides:
        count = lax.axis_size(axis)
        head = lax.slice_in_dim(cells, 0, width, axis=dim)
        tail = lax.slice_in_dim(cells, cells.shape[dim] - width, cells.shape[dim], axis=dim)
        cells = jnp.concatenate(
            [
                lax.ppermute(tail, axis, [(i, (i + 1) % count) for i in range(count)]),
                cells,
                lax.ppermute(head, axis, [((i + 1) % count, i) for i in range(count)]),
            ],
            axis=dim,
        )
    return cells


def spline_weights(frac):
    return (
        (0.5 - frac) * (0.5 - frac) * 0.5,
        0.75 - frac * frac,
        (0.5 + frac) * (0.5 + frac) * 0.5,
    )


def spline_slopes(frac):
    return (frac - 0.5, -2.0 * frac, 0.5 + frac)


def green_table(freq_x, freq_y, freq_z):

    def signed(frequency):
        return jnp.where(frequency < G // 2, frequency, frequency - G)

    signed_x = signed(freq_x)
    signed_y = signed(freq_y)
    signed_z = signed(freq_z)
    squares = signed_x * signed_x + signed_y * signed_y + signed_z * signed_z
    wave_sq = squares.astype(jnp.float32) * (2.0 * math.pi / G * (2.0 * math.pi / G))
    safe_sq = jnp.where(squares > 0, wave_sq, 1.0)
    return jnp.where(
        squares > 0, 4.0 * math.pi * jnp.exp(-wave_sq / (4.0 * EWALD * EWALD)) / safe_sq, 0.0
    )


def dft_tables():
    frequency = jnp.arange(G, dtype=jnp.int32)
    phases = (frequency[:, None] * frequency[None, :] % G).astype(jnp.float32) * (2.0 * math.pi / G)
    return (jnp.cos(phases), jnp.sin(phases))


def along_axis(values, table, axis_num):
    if axis_num == 0:
        return jnp.einsum("kx,xyz->kyz", table, values, precision=HIGHEST)
    if axis_num == 1:
        return jnp.einsum("xyz,yk->xkz", values, table, precision=HIGHEST)
    return jnp.einsum("xyz,zk->xyk", values, table, precision=HIGHEST)


def transform(real_part, imag_part, axis_num, cosine, sine_table, inverse):
    cos_real = along_axis(real_part, cosine, axis_num)
    sin_imag = along_axis(imag_part, sine_table, axis_num)
    cos_imag = along_axis(imag_part, cosine, axis_num)
    sin_real = along_axis(real_part, sine_table, axis_num)
    if inverse:
        return (cos_real - sin_imag, cos_imag + sin_real)
    return (cos_real + sin_imag, cos_imag - sin_real)


def weights_for(center, frac, length, wrap):
    rows_idx = jnp.arange(length, dtype=jnp.int32)[:, None]
    values = spline_weights(frac)
    slopes = spline_slopes(frac)
    weight = jnp.zeros((length, frac.shape[0]), jnp.float32)
    slope_sum = jnp.zeros((length, frac.shape[0]), jnp.float32)
    for shift_by in range(3):
        target = center + (shift_by - 1)
        if wrap:
            target = target % length
        hit_mask = (rows_idx == target[None, :]).astype(jnp.float32)
        weight = weight + hit_mask * values[shift_by][None, :]
        slope_sum = slope_sum + hit_mask * slopes[shift_by][None, :]
    return (weight, slope_sum)


def pair_terms(pos_i, pos_j, embed_i, embed_j, self_mask, w_radial, w_hidden, w_charge, w_energy):
    separation = pos_j[:, None, :] - pos_i[:, :, None]
    half_box = 0.5 * G
    separation = jnp.where(
        separation > half_box,
        separation - G,
        jnp.where(separation < -half_box, separation + G, separation),
    )
    distance = jnp.sqrt(jnp.sum(separation * separation, axis=0))
    scaled = distance / CUTOFF
    inside = 1.0 - scaled * scaled
    envelope = jnp.where(scaled < 1.0, inside * inside, 0.0)
    envelope = jnp.where(self_mask, 0.0, envelope)
    orders = jnp.arange(1, NBASIS + 1).astype(jnp.float32)
    radial = jnp.sinc(scaled[:, :, None] * orders)
    hidden_pre = (
        jnp.einsum("ijn,nd->ijd", radial, w_radial, precision=HIGHEST)
        + embed_i[:, None, :]
        + embed_j[None, :, :]
    )
    edge_feat = jax.nn.silu(hidden_pre).astype(jnp.bfloat16).reshape(-1, w_radial.shape[1])
    charge_pair = jnp.dot(edge_feat, w_charge, preferred_element_type=jnp.float32).reshape(
        envelope.shape
    )
    charge_rows = jnp.sum(envelope * charge_pair, axis=1)
    latent = jax.nn.silu(jnp.dot(edge_feat, w_hidden, preferred_element_type=jnp.float32)).astype(
        jnp.bfloat16
    )
    energy_pair = jnp.dot(latent, w_energy, preferred_element_type=jnp.float32).reshape(
        envelope.shape
    )
    energy_rows = jnp.sum(envelope * energy_pair, axis=1)
    return (energy_rows, charge_rows)


def on_device(
    cell_index,
    offsets,
    species,
    pair_blocks,
    counts,
    background,
    species_embed,
    neighbour_embed,
    w_radial,
    w_hidden,
    w_charge,
    w_energy,
):
    atom_count = cell_index.shape[1]
    block_count = atom_count // BLOCK
    sub_rows = min(BLOCK, 2048 // BLOCK)
    slab_rows = G // lax.axis_size("dom")
    quarter = G // lax.axis_size("grp")
    dom_id = lax.axis_index("dom")
    grp_id = lax.axis_index("grp")
    plane_rows = slab_rows + 2
    strip_rows = quarter + 2
    part_size = min(atom_count, 512)
    positions = cell_index.astype(jnp.float32) + offsets
    record = jnp.concatenate([positions, species.astype(jnp.float32)[None, :]], axis=0)
    extended = padded(record, (("dom", 1),), atom_count)
    ext_pos = extended[:3]
    kind_values = jnp.arange(NSPEC).astype(jnp.float32)
    own_embed = jnp.dot(
        (species.astype(jnp.float32)[:, None] == kind_values[None, :]).astype(jnp.float32),
        species_embed,
        precision=HIGHEST,
    )
    ext_embed = jnp.dot(
        (extended[3][:, None] == kind_values[None, :]).astype(jnp.float32),
        neighbour_embed,
        precision=HIGHEST,
    )

    def block_terms(block_i, block_j):
        start_j = block_j * BLOCK
        pos_j = lax.dynamic_slice_in_dim(ext_pos, start_j, BLOCK, 1)
        embed_j = lax.dynamic_slice_in_dim(ext_embed, start_j, BLOCK, 0)
        energy_parts = []
        charge_parts = []
        for row_start in range(0, BLOCK, sub_rows):
            start_i = block_i * BLOCK + row_start
            pos_i = lax.dynamic_slice_in_dim(positions, start_i, sub_rows, 1)
            embed_i = lax.dynamic_slice_in_dim(own_embed, start_i, sub_rows, 0)
            row_ids = row_start + jnp.arange(sub_rows, dtype=jnp.int32)
            self_mask = (block_j == block_count + block_i) & (
                row_ids[:, None] == jnp.arange(BLOCK, dtype=jnp.int32)[None, :]
            )
            energy_rows, charge_rows = pair_terms(
                pos_i, pos_j, embed_i, embed_j, self_mask, w_radial, w_hidden, w_charge, w_energy
            )
            energy_parts.append(energy_rows)
            charge_parts.append(charge_rows)
        return (jnp.concatenate(energy_parts), jnp.concatenate(charge_parts))

    local_x = cell_index[0] - slab_rows * dom_id + 1
    local_y = cell_index[1] - quarter * grp_id + 1
    cosine, sine_table = dft_tables()

    def take_part(array, part_index):
        return lax.dynamic_slice_in_dim(array, part_index * part_size, part_size, array.ndim - 1)

    def visit_slot(slot_num, running):
        energy_acc, charge_acc = running
        block_i = pair_blocks[slot_num, 0]
        block_j = pair_blocks[slot_num, 1]
        energy_blk, charge_blk = block_terms(block_i, block_j)
        row_start = block_i * BLOCK
        energy_acc = lax.dynamic_update_slice_in_dim(
            energy_acc,
            lax.dynamic_slice_in_dim(energy_acc, row_start, BLOCK, 0) + energy_blk,
            row_start,
            0,
        )
        charge_acc = lax.dynamic_update_slice_in_dim(
            charge_acc,
            lax.dynamic_slice_in_dim(charge_acc, row_start, BLOCK, 0) + charge_blk,
            row_start,
            0,
        )
        return (energy_acc, charge_acc)

    blank_row = jnp.zeros((atom_count,), jnp.float32)
    energies, charges = lax.fori_loop(0, counts[0], visit_slot, (blank_row, blank_row))

    def spread(part_index, region):
        weight_x, unused_x = weights_for(
            take_part(local_x, part_index), take_part(offsets[0], part_index), plane_rows, False
        )
        weight_y, unused_y = weights_for(
            take_part(local_y, part_index), take_part(offsets[1], part_index), strip_rows, False
        )
        weight_z, unused_z = weights_for(
            take_part(cell_index[2], part_index), take_part(offsets[2], part_index), G, True
        )
        mixture = (
            weight_x[:, None, :]
            * weight_y[None, :, :]
            * take_part(charges, part_index)[None, None, :]
        ).reshape(plane_rows * strip_rows, part_size)
        return region + jnp.einsum("ca,za->cz", mixture, weight_z, precision=HIGHEST)

    region = lax.fori_loop(
        0, atom_count // part_size, spread, jnp.zeros((plane_rows * strip_rows, G), jnp.float32)
    )
    region = region.reshape(plane_rows, strip_rows, G)
    region = region.at[1 : slab_rows + 1, 1 : quarter + 1].add(background)
    placed = jnp.zeros((plane_rows, G + 2, G), jnp.float32)
    placed = lax.dynamic_update_slice_in_dim(placed, region, quarter * grp_id, 1)
    full_rows = placed[:, 1 : G + 1]
    full_rows = full_rows.at[:, G - 1].add(placed[:, 0])
    full_rows = full_rows.at[:, 0].add(placed[:, G + 1])
    rim_pair = jnp.concatenate([full_rows[0:1], full_rows[plane_rows - 1 : plane_rows]], axis=0)
    arrived = padded(rim_pair, (("dom", 0),), 1)
    own_slab = full_rows[1 : plane_rows - 1]
    own_slab = own_slab.at[0].add(arrived[0])
    own_slab = own_slab.at[slab_rows - 1].add(arrived[3])
    low_row = (quarter * grp_id + G - 1) % G
    high_row = (quarter * grp_id + quarter) % G
    spill_rows = jnp.concatenate(
        [
            lax.dynamic_slice_in_dim(own_slab, low_row, 1, 1),
            lax.dynamic_slice_in_dim(own_slab, high_row, 1, 1),
        ],
        axis=1,
    )
    spill_in = padded(spill_rows, (("grp", 1),), 1)
    shared_rows = lax.dynamic_slice_in_dim(own_slab, quarter * grp_id, quarter, 1)
    shared_rows = shared_rows.at[:, 0].add(spill_in[:, 0])
    shared_rows = shared_rows.at[:, quarter - 1].add(spill_in[:, 3])
    real_part = along_axis(shared_rows, cosine, 2)
    imag_part = -along_axis(shared_rows, sine_table, 2)
    real_part, imag_part = (
        lax.all_to_all(real_part, "grp", split_axis=2, concat_axis=1, tiled=True),
        lax.all_to_all(imag_part, "grp", split_axis=2, concat_axis=1, tiled=True),
    )
    real_part, imag_part = transform(real_part, imag_part, 1, cosine, sine_table, False)
    real_part, imag_part = (
        lax.all_to_all(real_part, "dom", split_axis=1, concat_axis=0, tiled=True),
        lax.all_to_all(imag_part, "dom", split_axis=1, concat_axis=0, tiled=True),
    )
    real_part, imag_part = transform(real_part, imag_part, 0, cosine, sine_table, False)
    width_y = real_part.shape[1]
    width_z = real_part.shape[2]
    freq_y = dom_id * width_y + jnp.arange(width_y, dtype=jnp.int32)
    freq_z = grp_id * width_z + jnp.arange(width_z, dtype=jnp.int32)
    freq_full = jnp.arange(G, dtype=jnp.int32)
    green_vals = green_table(
        freq_full[:, None, None], freq_y[None, :, None], freq_z[None, None, :]
    ) / (G * G * G)
    real_part = real_part * green_vals
    imag_part = imag_part * green_vals
    real_part, imag_part = transform(real_part, imag_part, 0, cosine, sine_table, True)
    real_part, imag_part = (
        lax.all_to_all(real_part, "dom", split_axis=0, concat_axis=1, tiled=True),
        lax.all_to_all(imag_part, "dom", split_axis=0, concat_axis=1, tiled=True),
    )
    real_part, imag_part = transform(real_part, imag_part, 1, cosine, sine_table, True)
    real_part, imag_part = (
        lax.all_to_all(real_part, "grp", split_axis=1, concat_axis=2, tiled=True),
        lax.all_to_all(imag_part, "grp", split_axis=1, concat_axis=2, tiled=True),
    )
    potential_grid = along_axis(real_part, cosine, 2) - along_axis(imag_part, sine_table, 2)
    region_grid = padded(potential_grid, (("dom", 0), ("grp", 1)), 1)
    flat_grid = region_grid.reshape(plane_rows * strip_rows, G)

    def sample(part_index, running):
        potential, field_rows = running
        weight_x, slope_x = weights_for(
            take_part(local_x, part_index), take_part(offsets[0], part_index), plane_rows, False
        )
        weight_y, slope_y = weights_for(
            take_part(local_y, part_index), take_part(offsets[1], part_index), strip_rows, False
        )
        weight_z, slope_z = weights_for(
            take_part(cell_index[2], part_index), take_part(offsets[2], part_index), G, True
        )
        along_z = jnp.einsum("cz,za->ca", flat_grid, weight_z, precision=HIGHEST).reshape(
            plane_rows, strip_rows, part_size
        )
        slope_vals = jnp.einsum("cz,za->ca", flat_grid, slope_z, precision=HIGHEST).reshape(
            plane_rows, strip_rows, part_size
        )
        cross_xy = weight_x[:, None, :] * weight_y[None, :, :]
        sampled = jnp.sum(cross_xy * along_z, axis=(0, 1))
        grad_x = jnp.sum(slope_x[:, None, :] * weight_y[None, :, :] * along_z, axis=(0, 1))
        grad_y = jnp.sum(weight_x[:, None, :] * slope_y[None, :, :] * along_z, axis=(0, 1))
        grad_z = jnp.sum(cross_xy * slope_vals, axis=(0, 1))
        potential = lax.dynamic_update_slice_in_dim(potential, sampled, part_index * part_size, 0)
        field_rows = lax.dynamic_update_slice_in_dim(
            field_rows, -jnp.stack([grad_x, grad_y, grad_z], axis=0), part_index * part_size, 1
        )
        return (potential, field_rows)

    start_state = (jnp.zeros((atom_count,), jnp.float32), jnp.zeros((3, atom_count), jnp.float32))
    potential, electric_field = lax.fori_loop(0, atom_count // part_size, sample, start_state)
    site_energy = energies + 0.5 * charges * potential
    return (site_energy, electric_field, charges)


def solution(mesh):
    return jax.shard_map(
        on_device,
        mesh=mesh,
        in_specs=(
            P(None, ("grp", "dom")),
            P(None, ("grp", "dom")),
            P(("grp", "dom")),
            P(("grp", "dom"), None),
            P(("grp", "dom")),
            P("dom", "grp", None),
            P(),
            P(),
            P(),
            P(),
            P(),
            P(),
        ),
        out_specs=(P(("grp", "dom")), P(None, ("grp", "dom")), P(("grp", "dom"))),
        check_vma=False,
    )
```

profile of v0, /device:TPU:13, one launch (start us, length us, event | category | flops | bytes accessed | tf_op | source)
XLA Modules:
  0.0 1130.2 jit_solution(6279183618879539074)
XLA Ops:
  17.8 161.1 %while.56 = (s32[]{:T(128)}, f32[2048]{0:T(1024)}, f32[2048]{0:T(1024)}, s32[]{:T(128)}, s32[4,2]{0,1:T(2,128)}, /*index=5*/f32[3,6144]{1,0:T(4,128)}, f32[3,204...) while((s32[]{:T(128)}, f32[2048]{0:T(1024)}, ...), condition=%wide.region_25.27_spmd, body=%wide.region_0.26_spmd.sunk | while | flops 2622357760 | bytes 28654592 | solution.py:227
  178.9 68.9 %while.58 = (s32[]{:T(128)}, f32[2244,256]{1,0:T(8,128)S(1)}, s32[2048]{0:T(1024)}, f32[3,2048]{1,0:T(4,128)S(1)}, s32[2048]{0:T(1024)}, /*index=5*/f32[2048]{0:...) while((s32[]{:T(128)}, f32[2244,256]{1,0:T(8,128)S(1)}, ...), condition=%wide.region_27.29_spmd.clone, body=%wide.region_26.28_spmd.clone.sunk | while | flops 3534444032 | bytes 23550136 | solution.py:246
  190.0 6.2 fusion.967
  207.2 6.2 fusion.967
  224.4 6.2 fusion.967
  241.7 6.2 fusion.967
  253.8 10.2 scatter-add.24
  268.2 11.9 %dynamic_update_slice.39 = f32[34,258,256]{2,1,0:T(8,128)} dynamic-update-slice(f32[34,258,256]{2,1,0:T(8,128)} %broadcast_in_dim.296, f32[34,66,256]{2,1,0:T(8,128)S(1)} %scatter-add.24, s32[]{:T(128)} %constant.856.clone.1, s32[]{:T(128)S(6)} %select_n.555, s32[]{:T(128)} %constant.856.clone.1) | dynamic-update-slice | bytes 4595716 | tf_op jit(solution)/shard_map/dynamic_update_slice | solution.py:252
  280.0 8.3 slice.311
  295.9 73.6 %collective-permute-start.2 = (f32[1,256,256]{2,1,0:T(8,128)S(1)}, f32[1,256,256]{2,1,0:T(8,128)S(1)}, u32[]{:S(2)}, u32[]{:S(2)}) collective-permute-start(f32[1,256,256]{2,1,0:T(8,128)S(1)} %get-tuple-element.918), channel_id=1, source_target_pairs={{0,1},{1,2},{2,3},{3,4},{4,5},{5,6},{6,7},{7,0},{8,9},{9,10},{10,1... | collective-permute-start | bytes 786440 | tf_op jit(solution)/shard_map/ppermute | solution.py:26
  375.7 73.5 %collective-permute-start.4 = (f32[32,1,256]{2,1,0:T(1,128)S(1)}, f32[32,1,256]{2,1,0:T(1,128)S(1)}, u32[]{:S(2)}, u32[]{:S(2)}) collective-permute-start(f32[32,1,256]{2,1,0:T(1,128)S(1)} %get-tuple-element.920), channel_id=1, source_target_pairs={{0,8},{8,16},{16,24},{24,0},{1,9},{9,17},{17,25},{25,1},{2,10},{10... | collective-permute-start | bytes 98312 | tf_op jit(solution)/shard_map/ppermute | solution.py:26
  487.8 7.1 all-to-all-done
  494.9 6.1 all-to-all-start.1
  501.5 7.7 reduce.19
  513.2 6.9 copy.112
  528.7 9.0 reduce.18
  543.2 7.0 copy.111
  567.3 7.2 reshape.1386
  574.5 9.7 all-to-all-start.2
  596.2 7.2 reshape.1388
  603.4 26.4 %all-to-all-done.2 = f32[8,1,65536]{2,1,0:T(1,128)} async-done(((f32[8,1,65536]{2,1,0:T(1,128)}), f32[8,1,65536]{2,1,0:T(1,128)}, u32[]{:S(2)}, u32[]{:S(2)}) %all-to-all-start.2) | async-done | bytes 2097184 | tf_op jit(solution)/shard_map/all_to_all | solution.py:282
  629.8 7.1 all-to-all-start.3
  637.1 7.4 reduce.21
  648.1 6.5 copy.75
  666.7 15.9 %all-to-all-done.3 = f32[8,1,65536]{2,1,0:T(1,128)} async-done(((f32[8,1,65536]{2,1,0:T(1,128)}), f32[8,1,65536]{2,1,0:T(1,128)}, u32[]{:S(2)}, u32[]{:S(2)}) %all-to-all-start.3) | async-done | bytes 2097184 | tf_op jit(solution)/shard_map/all_to_all | solution.py:283
  682.6 7.4 reduce.20
  694.0 6.5 copy.79
  724.4 7.2 reshape.1392
  731.6 6.5 all-to-all-start.5
  750.1 7.2 reshape.1390
  757.3 26.4 %all-to-all-done.5 = f32[8,1,65536]{2,1,0:T(1,128)} async-done(((f32[8,1,65536]{2,1,0:T(1,128)}), f32[8,1,65536]{2,1,0:T(1,128)}, u32[]{:S(2)}, u32[]{:S(2)}) %all-to-all-start.5) | async-done | bytes 2097184 | tf_op jit(solution)/shard_map/all_to_all | solution.py:299
  783.8 6.7 all-to-all-start.4
  790.5 7.4 reduce.23
  813.6 22.5 %all-to-all-done.4 = f32[8,1,65536]{2,1,0:T(1,128)} async-done(((f32[8,1,65536]{2,1,0:T(1,128)}), f32[8,1,65536]{2,1,0:T(1,128)}, u32[]{:S(2)}, u32[]{:S(2)}) %all-to-all-start.4) | async-done | bytes 2097184 | tf_op jit(solution)/shard_map/all_to_all | solution.py:298
  836.1 8.5 reduce.22
  896.7 9.0 all-to-all-done.7
  911.2 7.7 reduce.25
  922.9 6.8 copy.109
  936.1 7.7 reduce.24
  947.7 6.9 copy.110
  980.2 149.0 %while.57 = (s32[]{:T(128)}, f32[2048]{0:T(1024)S(1)}, f32[3,2048]{1,0:T(4,128)S(1)}, s32[2048]{0:T(1024)}, f32[3,2048]{1,0:T(4,128)S(1)}, /*index=5*/s32[2048]{...) while((s32[]{:T(128)}, f32[2048]{0:T(1024)S(1)}, ...), condition=%wide.region_33.35_spmd, body=%wide.region_28.34_spmd.sunk | while | flops 7074452480 | bytes 79196392 | solution.py:339
  981.2 6.0 broadcast_multiply_fusion.9
  1005.0 7.9 multiply_reduce_fusion.36
  1042.2 7.9 multiply_reduce_fusion.36
  1055.8 6.0 broadcast_multiply_fusion.9
  1079.5 7.9 multiply_reduce_fusion.36
  1093.0 6.0 broadcast_multiply_fusion.9
  1116.7 7.9 multiply_reduce_fusion.36
  (500 shorter events, 574.7 us)
Async XLA Ops:
  0.6 9.8 copy-start
  3.5 6.1 collective-permute-start
  4.8 4.8 collective-permute-start.1
  17.8 161.1 %copy-start.2 = (f32[2244,256]{1,0:T(8,128)S(1)}, f32[2244,256]{1,0:T(8,128)}, u32[]{:S(2)}) copy-start(f32[2244,256]{1,0:T(8,128)} %custom-call) | copy-start | bytes 6893572
  17.8 161.1 %copy-start.11 = (f32[3,2048]{1,0:T(4,128)S(1)}, f32[3,2048]{1,0:T(4,128)}, u32[]{:S(2)}) copy-start(f32[3,2048]{1,0:T(4,128)} %param.34) | copy-start | bytes 73732
  43.6 3.0 copy-start.38
  43.6 3.0 copy-start.36
  43.6 4.5 copy-start.35
  54.5 3.0 copy-start.15
  70.8 3.0 copy-start.17
  78.6 3.0 copy-start.18
  78.6 4.0 copy-start.37
  114.9 3.0 copy-start.38
  114.9 4.5 copy-start.35
  125.8 3.0 copy-start.15
  134.3 3.0 copy-start.16
  142.1 3.0 copy-start.17
  149.9 3.0 copy-start.18
  149.9 4.0 copy-start.37
  249.6 4.2 copy-start.3
  295.9 77.5 %collective-permute-start.2 = (f32[1,256,256]{2,1,0:T(8,128)S(1)}, f32[1,256,256]{2,1,0:T(8,128)S(1)}, u32[]{:S(2)}, u32[]{:S(2)}) collective-permute-start(f32[1,256,256]{2,1,0:T(8,128)S(1)} %get-tuple-element.918), channel_id=1, source_target_pairs={{0,1},{1,2},{2,3},{3,4},{4,5},{5,6},{6,7},{7,0},{8,9},{9,10},{10,1... | collective-permute-start | bytes 786440 | tf_op jit(solution)/shard_map/ppermute | solution.py:26
  369.5 6.1 collective-permute-start.3
  375.7 74.5 %collective-permute-start.4 = (f32[32,1,256]{2,1,0:T(1,128)S(1)}, f32[32,1,256]{2,1,0:T(1,128)S(1)}, u32[]{:S(2)}, u32[]{:S(2)}) collective-permute-start(f32[32,1,256]{2,1,0:T(1,128)S(1)} %get-tuple-element.920), channel_id=1, source_target_pairs={{0,8},{8,16},{16,24},{24,0},{1,9},{9,17},{17,25},{25,1},{2,10},{10... | collective-permute-start | bytes 98312 | tf_op jit(solution)/shard_map/ppermute | solution.py:26
  449.3 3.4 collective-permute-start.5
  468.2 26.7 %all-to-all-start = ((f32[4,1,131072]{2,1,0:T(1,128)}), f32[4,1,131072]{2,1,0:T(1,128)}, u32[]{:S(2)}, u32[]{:S(2)}) async-start(f32[4,1,131072]{2,1,0:T(1,128)} %reshape.1382), calls=%async_computation | async-start | bytes 4194304 | tf_op jit(solution)/shard_map/all_to_all | solution.py:277
  494.9 33.8 %all-to-all-start.1 = ((f32[4,1,131072]{2,1,0:T(1,128)}), f32[4,1,131072]{2,1,0:T(1,128)}, u32[]{:S(2)}, u32[]{:S(2)}) async-start(f32[4,1,131072]{2,1,0:T(1,128)} %reshape.1384), calls=%async_computation.1 | async-start | bytes 4194304 | tf_op jit(solution)/shard_map/all_to_all | solution.py:278
  555.5 4.6 copy-start.9
  574.5 55.4 %all-to-all-start.2 = ((f32[8,1,65536]{2,1,0:T(1,128)}), f32[8,1,65536]{2,1,0:T(1,128)}, u32[]{:S(2)}, u32[]{:S(2)}) async-start(f32[8,1,65536]{2,1,0:T(1,128)} %reshape.1386), calls=%async_computation.2 | async-start | bytes 4194304 | tf_op jit(solution)/shard_map/all_to_all | solution.py:282
  629.8 52.8 %all-to-all-start.3 = ((f32[8,1,65536]{2,1,0:T(1,128)}), f32[8,1,65536]{2,1,0:T(1,128)}, u32[]{:S(2)}, u32[]{:S(2)}) async-start(f32[8,1,65536]{2,1,0:T(1,128)} %reshape.1388), calls=%async_computation.3 | async-start | bytes 4194304 | tf_op jit(solution)/shard_map/all_to_all | solution.py:283
  731.6 52.2 %all-to-all-start.5 = ((f32[8,1,65536]{2,1,0:T(1,128)}), f32[8,1,65536]{2,1,0:T(1,128)}, u32[]{:S(2)}, u32[]{:S(2)}) async-start(f32[8,1,65536]{2,1,0:T(1,128)} %reshape.1392), calls=%async_computation.5 | async-start | bytes 4194304 | tf_op jit(solution)/shard_map/all_to_all | solution.py:299
  783.8 52.4 %all-to-all-start.4 = ((f32[8,1,65536]{2,1,0:T(1,128)}), f32[8,1,65536]{2,1,0:T(1,128)}, u32[]{:S(2)}, u32[]{:S(2)}) async-start(f32[8,1,65536]{2,1,0:T(1,128)} %reshape.1390), calls=%async_computation.4 | async-start | bytes 4194304 | tf_op jit(solution)/shard_map/all_to_all | solution.py:298
  858.6 4.6 copy-start.10
  875.8 29.8 %all-to-all-start.7 = ((f32[4,1,131072]{2,1,0:T(1,128)}), f32[4,1,131072]{2,1,0:T(1,128)}, u32[]{:S(2)}, u32[]{:S(2)}) async-start(f32[4,1,131072]{2,1,0:T(1,128)} %reshape.1396), calls=%async_computation.7 | async-start | bytes 4194304 | tf_op jit(solution)/shard_map/all_to_all | solution.py:304
  905.7 30.4 %all-to-all-start.6 = ((f32[4,1,131072]{2,1,0:T(1,128)}), f32[4,1,131072]{2,1,0:T(1,128)}, u32[]{:S(2)}, u32[]{:S(2)}) async-start(f32[4,1,131072]{2,1,0:T(1,128)} %reshape.1394), calls=%async_computation.6 | async-start | bytes 4194304 | tf_op jit(solution)/shard_map/all_to_all | solution.py:303
  964.7 3.2 collective-permute-start.6
  966.0 4.0 collective-permute-start.7
  970.0 3.4 collective-permute-start.8
  972.4 3.4 collective-permute-start.9
  980.2 149.1 %copy-start.19 = (f32[2048]{0:T(1024)S(1)}, f32[2048]{0:T(1024)}, u32[]{:S(2)}) copy-start(f32[2048]{0:T(1024)} %get-tuple-element.1492) | copy-start | bytes 24580
  980.2 149.1 %copy-start.33 = (f32[2048]{0:T(1024)S(1)}, f32[2048]{0:T(1024)}, u32[]{:S(2)}) copy-start(f32[2048]{0:T(1024)} %get-tuple-element.718) | copy-start | bytes 24580
  1004.9 7.9 slice-start
  1005.0 7.9 slice-start.1
  1042.2 7.9 slice-start
  1042.2 7.9 slice-start.1
  1079.5 7.9 slice-start
  1079.5 7.9 slice-start.1
  1116.7 7.9 slice-start
  1116.7 7.9 slice-start.1
  (40 other events, 83.0 us)
where the time goes:
time: 1140 us; the launch traced here: 1130 us
  local copies, waits for them, and re-layouts  375 us (33%)
  matrix products  247 us (22%)
  starting transfers between devices  204 us (18%)
  other arithmetic  157 us (14%)
  waiting for transfers between devices  119 us (10%)
  loops' own time  26.7 us (2%)
    ppermute x5, starting transfers between devices, padded(): lax.ppermute(tail, axis, [(i, (i + 1) % count) for i in range(count)])  152 us
    unnamed x48, local copies, waits for them, and re-layouts  84.6 us
    unnamed x16, matrix products  57.3 us
    dot_general x16, matrix products, pair_terms(): jnp.einsum('ijn,nd->ijd', radial, w_radial, precision=HIGHEST)  47.7 us
    dot_general x16, matrix products, pair_terms(): jnp.dot(latent, w_energy, preferred_element_type=jnp.float32)  34.9 us
    dot_general x4, matrix products, sample(): jnp.einsum('cz,za->ca', flat_grid, weight_z, precision=HIGHEST)  31.5 us
    all_to_all x1, waiting for transfers between devices, on_device(): lax.all_to_all(imag_part, 'dom', split_axis=0, concat_axis=1, tiled=True)  26.4 us
    all_to_all x1, waiting for transfers between devices, on_device(): lax.all_to_all(real_part, 'dom', split_axis=1, concat_axis=0, tiled=True)  26.4 us
  transfers between devices with their start and end apart: 18, of which 14 were waited for; matrix products, arithmetic and copies ran while one was open for 15% of the time, Pallas kernels for 0%

commit v1 on v0

v1 whole, which is shorter than its diff:
```python
import functools
import math

import jax
import jax.numpy as jnp
import ml_dtypes
import numpy as np
from jax import lax
from jax.experimental import pallas as pl
from jax.experimental.pallas import tpu as pltpu
from jax.sharding import PartitionSpec as P

G = 256
NBASIS = 8
NSPEC = 8
BLOCK = 128
TILES_Y = 4
CUTOFF = 6.0
EWALD = 1.0
VMEM_BYTES = 56 << 20

BF = jnp.bfloat16
F32 = jnp.float32


def np_split(table):
    table = np.asarray(table, np.float32)
    high = table.astype(ml_dtypes.bfloat16)
    low = (table - high.astype(np.float32)).astype(ml_dtypes.bfloat16)
    return high, low


def hartley(points):
    phase = (np.arange(G)[:, None] * np.asarray(points)[None, :]) % G
    angle = phase.astype(np.float64) * (2.0 * math.pi / G)
    return np.cos(angle) + np.sin(angle)


def split2(x):
    high = x.astype(BF)
    low = (x - high.astype(F32)).astype(BF)
    return high, low


def dot_nn(a, b):
    return lax.dot_general(a, b, (((1,), (0,)), ((), ())), preferred_element_type=F32)


def dot_nt(a, b):
    return lax.dot_general(a, b, (((1,), (1,)), ((), ())), preferred_element_type=F32)


def dot3(dot, a, b):
    return dot(a[0], b[0]) + (dot(a[0], b[1]) + dot(a[1], b[0]))


def rounded(x):
    return lax.reduce_precision(x, exponent_bits=8, mantissa_bits=7)


def split3_outer(x):
    one = rounded(x)
    two = rounded(x - one)
    return one, two, rounded(x - one - two)


def split3(x):
    one = x.astype(BF).astype(F32)
    two = (x - one).astype(BF).astype(F32)
    three = (x - one - two).astype(BF).astype(F32)
    return one, two, three


def pair_kernel(
    slots, live, cols, ext, wcat, whid, wq, we, energy, charge, env_s, feat_s, kind_s, pq_s, pe_s, *, step
):
    blocks = energy.shape[0]
    energy[...] = jnp.zeros_like(energy)
    charge[...] = jnp.zeros_like(charge)
    half = 0.5 * G
    row8 = lax.broadcasted_iota(jnp.int32, (NSPEC, BLOCK), 0).astype(F32)
    diag = lax.broadcasted_iota(jnp.int32, (BLOCK, BLOCK), 0) == lax.broadcasted_iota(
        jnp.int32, (BLOCK, BLOCK), 1
    )

    def slot_body(slot, unused):
        bi = slots[slot, 0]
        bj = slots[slot, 1]
        ci = cols[pl.ds(pl.multiple_of(bi * BLOCK, BLOCK), BLOCK), :]
        rj = ext[:, pl.ds(pl.multiple_of(bj * BLOCK, BLOCK), BLOCK)]
        total = jnp.zeros((BLOCK, BLOCK), F32)
        for c in range(3):
            sep = rj[c : c + 1, :] - ci[:, c : c + 1]
            sep = jnp.where(sep > half, sep - G, jnp.where(sep < -half, sep + G, sep))
            total = total + sep * sep
        scaled = jnp.sqrt(total) / CUTOFF
        inside = 1.0 - scaled * scaled
        env = jnp.where(scaled < 1.0, inside * inside, 0.0)
        env = jnp.where(diag & (bj == blocks + bi), 0.0, env)
        env_s[...] = env
        kind_s[...] = jnp.broadcast_to(ci[:, 3:4], (BLOCK, BLOCK))
        theta = math.pi * jnp.minimum(scaled, 1.0)
        small = theta == 0.0
        inv = 1.0 / jnp.where(small, 1.0, theta)
        twice = 2.0 * jnp.cos(theta)
        before = jnp.zeros_like(theta)
        now = jnp.sin(theta)
        for n in range(1, NBASIS + 1):
            feat_s[pl.ds(n - 1, BLOCK, stride=NBASIS), :] = jnp.where(
                small, 1.0, now * inv * (1.0 / n)
            )
            before, now = now, twice * now - before
        kind_j = (row8 == rj[3:4, :]).astype(F32)

        def rows_body(it, unused_rows):
            i0 = it * step
            parts = []
            for k in range(step):
                i = i0 + k
                rad = feat_s[pl.ds(pl.multiple_of(i * NBASIS, NBASIS), NBASIS), :]
                one, two, three = split3(rad)
                kind_i = (row8 == kind_s[pl.ds(i, 1), :]).astype(F32)
                parts.append(
                    jnp.concatenate(
                        [one, one, one, two, two, three, kind_j, kind_j, kind_j, kind_i, kind_i, kind_i],
                        axis=0,
                    ).astype(BF)
                )
            feats = jnp.concatenate(parts, axis=1)
            h = dot_nn(wcat[...], feats)
            edge = (h + h * jnp.tanh(h)).astype(BF)
            cp = dot_nn(wq[...], edge)
            g = dot_nn(whid[...], edge)
            latent = (g + g * jnp.tanh(g)).astype(BF)
            ep = dot_nn(we[...], latent)
            for k in range(step):
                row = pl.ds(i0 + k, 1)
                env_row = env_s[row, :]
                pq_s[row, :] = env_row * cp[0:1, k * BLOCK : (k + 1) * BLOCK]
                pe_s[row, :] = env_row * ep[0:1, k * BLOCK : (k + 1) * BLOCK]
            return unused_rows

        lax.fori_loop(0, BLOCK // step, rows_body, 0)
        where = pl.ds(bi, 1)
        charge[where, :] = charge[where, :] + jnp.sum(pq_s[...].T, axis=0, keepdims=True)
        energy[where, :] = energy[where, :] + jnp.sum(pe_s[...].T, axis=0, keepdims=True)
        return unused

    lax.fori_loop(0, live[0], slot_body, 0)


def spline_rows(rows, first, center, frac, wrap, slopes):
    index = lax.broadcasted_iota(jnp.int32, (rows, frac.shape[1]), 0) + first
    if slopes:
        values = (frac - 0.5, -2.0 * frac, 0.5 + frac)
    else:
        values = ((0.5 - frac) * (0.5 - frac) * 0.5, 0.75 - frac * frac, (0.5 + frac) * (0.5 + frac) * 0.5)
    out = jnp.zeros((rows, frac.shape[1]), F32)
    for o in range(3):
        target = center + (o - 1)
        if wrap:
            target = jnp.where(target < 0, target + G, jnp.where(target >= G, target - G, target))
        out = jnp.where(index == target, values[o], out)
    return out


def chunk_blocks(blocks):
    per_tile = blocks // TILES_Y
    return [
        (t, [t + TILES_Y * z for z in range(2 * pair, 2 * pair + 2)])
        for t in range(TILES_Y)
        for pair in range(per_tile // 2)
    ]


def lanes_of(ref, row, pair):
    return jnp.concatenate([ref[row : row + 1, b * BLOCK : (b + 1) * BLOCK] for b in pair], axis=1)


def rows_of(ref, pair):
    return jnp.concatenate([ref[b : b + 1, :] for b in pair], axis=1)


def spread_kernel(local, frac, charge, back, hz_hi, hz_lo, out, acc):
    planes, padded_y, unused_z = acc.shape
    slab, quarter = back.shape[0], back.shape[1]
    window = 24
    tile = quarter // TILES_Y
    groups = out.shape[0]
    acc[...] = jnp.zeros_like(acc)
    acc[1 : slab + 1, 1 : quarter + 1, :] = back[...]
    for t, pair in chunk_blocks(charge.shape[0]):
        wx = spline_rows(planes, 0, lanes_of(local, 0, pair), lanes_of(frac, 0, pair), False, False)
        wy = spline_rows(window, tile * t, lanes_of(local, 1, pair), lanes_of(frac, 1, pair), False, False)
        wz = spline_rows(G, 0, lanes_of(local, 2, pair), lanes_of(frac, 2, pair), True, False)
        wy = wy * rows_of(charge, pair)
        mix = jnp.concatenate([wx[x : x + 1, :] * wy for x in range(planes)], axis=0)
        part = dot3(dot_nt, split2(mix), split2(wz))
        acc[:, tile * t : tile * t + window, :] += part.reshape(planes, window, G)
    low_half = lax.broadcasted_iota(jnp.int32, (padded_y, BLOCK), 1) < BLOCK // 2
    table = (hz_hi[...], hz_lo[...])
    for q in range(planes // 2):
        two = split2(acc[2 * q : 2 * q + 2].reshape(2 * padded_y, G))
        both = dot3(dot_nn, two, table)
        for s in range(groups):
            piece = both[:, s * BLOCK : (s + 1) * BLOCK]
            out[s, q] = jnp.where(low_half, piece[:padded_y], piece[padded_y:])


def y_kernel(data, hy_hi, hy_lo, out):
    groups, pairs = data.shape[0], data.shape[1]
    parts, rows = out.shape[0], out.shape[2]
    table = (hy_hi[...], hy_lo[...])
    for q in range(pairs):
        column = jnp.concatenate([data[g, q] for g in range(groups)], axis=0)
        result = dot3(dot_nn, table, split2(column))
        for d in range(parts):
            out[d, q] = result[d * rows : (d + 1) * rows]


def x_kernel(place, data, hx_hi, hx_lo, ix_hi, ix_lo, out, *, width_y):
    lines = data.shape[0] // width_y
    lane = lax.broadcasted_iota(jnp.int32, (lines, BLOCK), 1)
    low_half = lane < BLOCK // 2
    forward = (hx_hi[...], hx_lo[...])
    back = (ix_hi[...], ix_lo[...])
    grp_id = place[0]
    dom_id = place[1]

    def signed(m):
        return jnp.where(m < G // 2, m, m - G)

    shape = (G, BLOCK)
    mx = signed(lax.broadcasted_iota(jnp.int32, shape, 0))
    lanes = lax.broadcasted_iota(jnp.int32, shape, 1)
    in_high = lanes >= BLOCK // 2
    mz = signed(grp_id * (BLOCK // 2) + jnp.where(in_high, lanes - BLOCK // 2, lanes))
    base_sq = mx * mx + mz * mz
    unit = 2.0 * math.pi / G * (2.0 * math.pi / G)
    for pair in range(width_y // 2):
        first = pl.ds(2 * pair, lines, stride=width_y)
        second = pl.ds(2 * pair + 1, lines, stride=width_y)
        one = data[first, :]
        two = data[second, :]
        even = jnp.where(low_half, one, pltpu.roll(two, BLOCK // 2, 1))
        odd = jnp.where(low_half, pltpu.roll(one, BLOCK // 2, 1), two)
        column = jnp.concatenate([even, odd], axis=0)
        spectrum = dot3(dot_nn, forward, split2(column))
        my = signed(dom_id * width_y + 2 * pair + in_high.astype(jnp.int32))
        squares = base_sq + my * my
        wave = squares.astype(F32) * unit
        safe = jnp.where(squares > 0, wave, 1.0)
        green = jnp.where(
            squares > 0, 4.0 * math.pi * jnp.exp(-wave / (4.0 * EWALD * EWALD)) / safe, 0.0
        ) * (1.0 / (G * G * G))
        result = dot3(dot_nn, back, split2(spectrum * green))
        even = result[:lines]
        odd = result[lines:]
        out[first, :] = jnp.where(low_half, even, pltpu.roll(odd, BLOCK // 2, 1))
        out[second, :] = jnp.where(low_half, pltpu.roll(even, BLOCK // 2, 1), odd)


def sample_kernel(local, frac, charge, energy, data, hz_hi, hz_lo, site, field, mesh_s):
    planes, padded_y, unused_z = mesh_s.shape
    groups = data.shape[0]
    window = 24
    tile = (G // groups) // TILES_Y
    low_half = lax.broadcasted_iota(jnp.int32, (padded_y, BLOCK), 1) < BLOCK // 2
    table = (hz_hi[...], hz_lo[...])
    for q in range(planes // 2):
        evens = []
        odds = []
        for h in range(groups // 2):
            one = data[2 * h, q]
            two = data[2 * h + 1, q]
            evens.append(jnp.where(low_half, one, pltpu.roll(two, BLOCK // 2, 1)))
            odds.append(jnp.where(low_half, pltpu.roll(one, BLOCK // 2, 1), two))
        both = jnp.concatenate(
            [jnp.concatenate(evens, axis=1), jnp.concatenate(odds, axis=1)], axis=0
        )
        mesh_s[2 * q : 2 * q + 2] = dot3(dot_nn, split2(both), table).reshape(2, padded_y, G)
    for t, pair in chunk_blocks(charge.shape[0]):
        lx, fx = lanes_of(local, 0, pair), lanes_of(frac, 0, pair)
        ly, fy = lanes_of(local, 1, pair), lanes_of(frac, 1, pair)
        lz, fz = lanes_of(local, 2, pair), lanes_of(frac, 2, pair)
        wx = spline_rows(planes, 0, lx, fx, False, False)
        sx = spline_rows(planes, 0, lx, fx, False, True)
        wy = spline_rows(window, tile * t, ly, fy, False, False)
        sy = spline_rows(window, tile * t, ly, fy, False, True)
        wz = spline_rows(G, 0, lz, fz, True, False)
        sz = spline_rows(G, 0, lz, fz, True, True)
        strip = split2(mesh_s[:, tile * t : tile * t + window, :].reshape(planes * window, G))
        along = dot3(dot_nn, strip, split2(wz))
        slope = dot3(dot_nn, strip, split2(sz))
        value_y = jnp.zeros_like(wy)
        grad_y = jnp.zeros_like(wy)
        slope_y = jnp.zeros_like(wy)
        for x in range(planes):
            here = along[x * window : (x + 1) * window]
            value_y = value_y + wx[x : x + 1] * here
            grad_y = grad_y + sx[x : x + 1] * here
            slope_y = slope_y + wx[x : x + 1] * slope[x * window : (x + 1) * window]
        pot = jnp.sum(wy * value_y, axis=0, keepdims=True)
        rows = [
            -jnp.sum(wy * grad_y, axis=0, keepdims=True),
            -jnp.sum(sy * value_y, axis=0, keepdims=True),
            -jnp.sum(wy * slope_y, axis=0, keepdims=True),
        ]
        result = rows_of(energy, pair) + 0.5 * rows_of(charge, pair) * pot
        for k, b in enumerate(pair):
            cut = slice(k * BLOCK, (k + 1) * BLOCK)
            site[b : b + 1, :] = result[:, cut]
            for c in range(3):
                field[c : c + 1, b * BLOCK : (b + 1) * BLOCK] = rows[c][:, cut]


VMEM_SPEC = pl.BlockSpec(memory_space=pltpu.VMEM)
SMEM_SPEC = pl.BlockSpec(memory_space=pltpu.SMEM)


def call(body, outs, scratch, scalars, args):
    specs = [SMEM_SPEC] * scalars + [VMEM_SPEC] * (len(args) - scalars)
    many = isinstance(outs, (list, tuple))
    return pl.pallas_call(
        body,
        out_shape=outs,
        in_specs=specs,
        out_specs=[VMEM_SPEC] * len(outs) if many else VMEM_SPEC,
        scratch_shapes=scratch,
        compiler_params=pltpu.CompilerParams(vmem_limit_bytes=VMEM_BYTES),
    )(*args)


def pair_weights(species_embed, neighbour_embed, w_radial, w_hidden, w_charge, w_energy):
    r1, r2, r3 = split3_outer(w_radial)
    table = jnp.concatenate(
        [r1, r2, r3, r1, r2, r1, *split3_outer(neighbour_embed), *split3_outer(species_embed)], axis=0
    )
    wcat = (0.5 * table).T.astype(BF)
    whid = (0.5 * w_hidden.astype(F32)).T.astype(BF)
    width = w_charge.shape[0]
    wq = jnp.broadcast_to(w_charge[None, :], (16, width))
    we = jnp.broadcast_to(w_energy[None, :], (16, width))
    return wcat, whid, wq, we


def pair_call(pair_blocks, counts, record, extended, weights, blocks):
    cols = jnp.pad(record.T, ((0, 0), (0, 4)))
    shape = jax.ShapeDtypeStruct((blocks, BLOCK), F32)
    square = pltpu.VMEM((BLOCK, BLOCK), F32)
    return call(
        functools.partial(pair_kernel, step=4),
        [shape, shape],
        [square, pltpu.VMEM((BLOCK * NBASIS, BLOCK), F32), square, square, square],
        2,
        (pair_blocks, counts, cols, extended, *weights),
    )


def tables(slab, quarter, doms, groups, padded_y):
    planes = slab + 2
    points = np.arange(G)
    plain = hartley(points)
    half = G // groups
    order = np.concatenate([np.tile(np.arange(s * half, (s + 1) * half), 2) for s in range(groups)])
    hz_dup = plain[order].T
    hz_inv = plain
    y_points = np.array([quarter * g - 1 + r for g in range(groups) for r in range(padded_y)]) % G
    y_used = np.array([r < quarter + 2 for g in range(groups) for r in range(padded_y)])
    hy = hartley(y_points) * y_used[None, :]
    x_points = np.array(
        [slab * d - 1 + 2 * q + par for par in range(2) for d in range(doms) for q in range(planes // 2)]
    ) % G
    hx = hartley(x_points)
    return [np_split(t) for t in (hz_dup, hz_inv, hy, hy.T, hx, hx.T)]


def on_device(
    cell_index,
    offsets,
    species,
    pair_blocks,
    counts,
    background,
    species_embed,
    neighbour_embed,
    w_radial,
    w_hidden,
    w_charge,
    w_energy,
):
    atoms = cell_index.shape[1]
    blocks = atoms // BLOCK
    doms = lax.axis_size("dom")
    groups = lax.axis_size("grp")
    slab = G // doms
    quarter = G // groups
    planes = slab + 2
    pairs = planes // 2
    padded_y = quarter + 8
    width_y = G // doms
    dom_id = lax.axis_index("dom")
    grp_id = lax.axis_index("grp")
    hz_dup, hz_inv, hy, hy_inv, hx, hx_inv = tables(slab, quarter, doms, groups, padded_y)

    positions = cell_index.astype(F32) + offsets
    record = jnp.concatenate([positions, species.astype(F32)[None, :]], axis=0)
    left = lax.ppermute(record, "dom", [(i, (i + 1) % doms) for i in range(doms)])
    right = lax.ppermute(record, "dom", [((i + 1) % doms, i) for i in range(doms)])
    extended = jnp.concatenate([left, record, right], axis=1)
    weights = pair_weights(species_embed, neighbour_embed, w_radial, w_hidden, w_charge, w_energy)
    energies, charges = pair_call(pair_blocks, counts, record, extended, weights, blocks)

    origin = jnp.stack([1 - slab * dom_id, 1 - quarter * grp_id, jnp.zeros_like(dom_id)])
    local = cell_index + origin[:, None]
    spec = call(
        spread_kernel,
        jax.ShapeDtypeStruct((groups, pairs, padded_y, BLOCK), F32),
        [pltpu.VMEM((planes, padded_y, G), F32)],
        0,
        (local, offsets, charges, background, *hz_dup),
    )
    spec = lax.all_to_all(spec, "grp", 0, 0, tiled=True)
    spec = call(
        y_kernel, jax.ShapeDtypeStruct((doms, pairs, width_y, BLOCK), F32), [], 0, (spec, *hy)
    )
    spec = lax.all_to_all(spec, "dom", 0, 0, tiled=True)
    place = jnp.stack([grp_id, dom_id]).astype(jnp.int32)
    spec = call(
        functools.partial(x_kernel, width_y=width_y),
        jax.ShapeDtypeStruct((doms * pairs * width_y, BLOCK), F32),
        [],
        1,
        (place, spec.reshape(doms * pairs * width_y, BLOCK), *hx, *hx_inv),
    )
    spec = lax.all_to_all(spec.reshape(doms, pairs, width_y, BLOCK), "dom", 0, 0, tiled=True)
    spec = call(
        y_kernel, jax.ShapeDtypeStruct((groups, pairs, padded_y, BLOCK), F32), [], 0, (spec, *hy_inv)
    )
    spec = lax.all_to_all(spec, "grp", 0, 0, tiled=True)
    site, field = call(
        sample_kernel,
        [jax.ShapeDtypeStruct((blocks, BLOCK), F32), jax.ShapeDtypeStruct((3, atoms), F32)],
        [pltpu.VMEM((planes, padded_y, G), F32)],
        0,
        (local, offsets, charges, energies, spec, *hz_inv),
    )
    return (site.reshape(atoms), field, charges.reshape(atoms))


def solution(mesh):
    return jax.shard_map(
        on_device,
        mesh=mesh,
        in_specs=(
            P(None, ("grp", "dom")),
            P(None, ("grp", "dom")),
            P(("grp", "dom")),
            P(("grp", "dom"), None),
            P(("grp", "dom")),
            P("dom", "grp", None),
            P(),
            P(),
            P(),
            P(),
            P(),
            P(),
        ),
        out_specs=(P(("grp", "dom")), P(None, ("grp", "dom")), P(("grp", "dom"))),
        check_vma=False,
    )
```

time: 1140 us -> 322 us (0.28)
  local copies, waits for them, and re-layouts: 375 us -> 8.9 us
  matrix products: 247 us -> 0 us
  starting transfers between devices: 204 us -> 26.3 us
  blocking collectives: 0 us -> 163 us
  other arithmetic: 157 us -> 7.75 us
  waiting for transfers between devices: 119 us -> 47.9 us
  Pallas kernels: 0 us -> 63 us
  loops' own time: 26.7 us -> 0 us
    dot_general x66 -> x0, matrix products: 190 us -> none  [the longest x16 47.7 us: pair_terms(): jnp.einsum('ijn,nd->ijd', radial, w_radial, precision=HIGHEST)]
    all_to_all x0 -> x3, blocking collectives: none -> 163 us  [the longest x2 108 us: on_device(): spec = lax.all_to_all(spec, 'grp', 0, 0, tiled=True)]
    ppermute x10 -> x2, starting transfers between devices: 153 us -> 1.52 us  [the longest x1 1.29 us: on_device(): lax.ppermute(record, 'dom', [(i, (i + 1) % doms) for i in range(doms)])]
    mul x16 -> x0, local copies, waits for them, and re-layouts: 90.2 us -> none  [the longest x4 22.6 us: sample(): slope_x[:, None, :] * weight_y[None, :, :] * along_z]
    all_to_all x17 -> x0, local copies, waits for them, and re-layouts: 84.9 us -> none  [the longest x3 12.8 us: on_device(): lax.all_to_all(imag_part, 'grp', split_axis=2, concat_axis=1, tiled=True)]
    unnamed x48 -> x14, local copies, waits for them, and re-layouts: 84.6 us -> 5.83 us
    all_to_all x8 -> x0, other arithmetic: 63 us -> none  [the longest x1 9.04 us: on_device(): lax.all_to_all(imag_part, 'grp', split_axis=2, concat_axis=1, tiled=True)]
    pallas_call x0 -> x6, Pallas kernels: none -> 63 us  [call(): pl.pallas_call(body, out_shape=outs, in_specs=specs, out_specs=[VMEM_SPEC...]
  transfers between devices with their start and end apart: 18 -> 3, of which waited for: 14 -> 1; matrix products, arithmetic and copies ran while one was open for 15% -> 4% of each run, Pallas kernels for 0% -> 0%
where the time goes in v1:
time: 322 us; the launch traced here: 318 us
  blocking collectives  163 us (51%)
  Pallas kernels  63 us (20%)
  waiting for transfers between devices  47.9 us (15%)
  starting transfers between devices  26.3 us (8%)
  local copies, waits for them, and re-layouts  8.9 us (3%)
  other arithmetic  7.75 us (2%)
    all_to_all x2, blocking collectives, on_device(): spec = lax.all_to_all(spec, 'grp', 0, 0, tiled=True)  108 us
    pallas_call x6, Pallas kernels, call(): pl.pallas_call(body, out_shape=outs, in_specs=specs, out_specs=[VMEM_SPEC...  63 us
    all_to_all x1, blocking collectives, on_device(): lax.all_to_all(spec.reshape(doms, pairs, width_y, BLOCK), 'dom', 0, 0, ti...  54.9 us
    all_to_all x1, waiting for transfers between devices, on_device(): spec = lax.all_to_all(spec, 'dom', 0, 0, tiled=True)  47.9 us
    all_to_all x1, starting transfers between devices, on_device(): spec = lax.all_to_all(spec, 'dom', 0, 0, tiled=True)  24.8 us
  transfers between devices with their start and end apart: 3, of which 1 were waited for; matrix products, arithmetic and copies ran while one was open for 4% of the time, Pallas kernels for 0%

profile of v1, /device:TPU:13, one launch (start us, length us, event | category | flops | bytes accessed | tf_op | source)
XLA Modules:
  0.0 317.8 jit_solution(14336595298431896061)
XLA Ops:
  0.6 0.7 convert_element_type.22
  1.3 0.8 convert_add_fusion
  2.1 1.3 collective-permute-start
  3.4 0.2 collective-permute-start.1
  3.7 0.7 reduce_precision.33
  4.4 0.8 copy.40
  5.2 0.7 reduce_precision.30
  5.9 0.8 copy.38
  6.7 0.7 reduce_precision.27
  7.4 0.8 copy.36
  8.3 0.1 pad_add_fusion
  8.3 1.4 broadcast_add_fusion.local
  9.8 0.0 copy-start.1
  9.8 0.1 copy.42
  9.9 0.1 copy.45
  10.0 0.1 copy.46
  10.2 1.0 copy.47
  11.2 0.7 fusion.whid
  11.9 0.5 concatenate.11
  12.4 0.0 copy-start.2
  12.4 0.0 copy-start.3
  12.4 0.6 fusion.1.wcat
  13.7 0.0 copy-done.1
  13.7 0.7 copy.48.slots
  14.4 0.4 copy.50
  14.7 1.0 pad.4.clone.cols
  15.8 0.0 collective-permute-done
  15.8 0.0 collective-permute-done.1
  15.8 0.7 pad_maximum_fusion.ext
  16.5 0.0 copy-done.2
  16.5 0.6 broadcast_in_dim.7.wq
  17.1 0.0 copy-done.3
  17.1 0.6 broadcast_in_dim.8.we
  17.7 21.2 %shard_map.247 = (f32[16,128]{1,0:T(8,128)}, f32[16,128]{1,0:T(8,128)}) custom-call(s32[4,2]{1,0:T(4,128)} %copy.48.slots, s32[1]{0:T(128)S(6)} %copy.51.live, f32[2048,8]{1,0:T(8,128)} %pad.4.clone.cols, f32[4,6144]{1,0:T(4,128)} %pad_maximum_fusion.ext, bf16[256,96]{1,0:T(8,128)(2,1)} %fusion.1.wcat, bf16[256,256]{1,0:T(8,128)(2,1)} %fusion.whid, ...), custom_call_target="tpu_custom_call" | custom-call | tf_op jit(solution)/shard_map/pallas_call | solution.py:324
  38.8 8.7 %shard_map.248 = f32[4,17,72,128]{3,2,1,0:T(8,128)} custom-call(s32[3,2048]{1,0:T(4,128)} %broadcast_add_fusion.local, f32[3,2048]{1,0:T(4,128)} %frac.3, f32[16,128]{1,0:T(8,128)} %get-tuple-element.7.charge, f32[32,64,256]{2,1,0:T(8,128)} %back.1, bf16[256,512]{1,0:T(8,128)(2,1)} %constant.46.clone.hz_hi, bf16[256,512]{1,0:T(8,128)(2,1)} %constant.47.clone.hz_lo), custom_call_target="tpu_custom_call" | custom-call | tf_op jit(solution)/shard_map/pallas_call | solution.py:324
  47.5 71.5 %all_to_all.20.data = f32[4,17,72,128]{3,2,1,0:T(8,128)} all-to-all(f32[4,17,72,128]{3,2,1,0:T(8,128)} %shard_map.248), channel_id=1, replica_groups=mesh['grp'=4,'dom'=8] {'grp'}, dimensions={0} | all-to-all | bytes 5013504 | tf_op jit(solution)/shard_map/all_to_all | solution.py:423
  119.0 5.9 %shard_map.249 = f32[8,17,32,128]{3,2,1,0:T(8,128)} custom-call(f32[4,17,72,128]{3,2,1,0:T(8,128)} %all_to_all.20.data, bf16[256,288]{1,0:T(8,128)(2,1)} %constant.48.clone.hy_hi, bf16[256,288]{1,0:T(8,128)(2,1)} %constant.49.clone.hy_lo), custom_call_target="tpu_custom_call" | custom-call | tf_op jit(solution)/shard_map/pallas_call | solution.py:324
  125.0 24.8 %all-to-all-start.1 = ((f32[8,17,32,128]{3,2,1,0:T(8,128)}), f32[8,17,32,128]{3,2,1,0:T(8,128)S(1)}, u32[]{:S(2)}, u32[]{:S(2)}) async-start(f32[8,17,32,128]{3,2,1,0:T(8,128)} %shard_map.249), calls=%async_computation.1 | async-start | bytes 4456448 | tf_op jit(solution)/shard_map/all_to_all | solution.py:427
  149.7 0.6 pad_add_fusion.1.place
  150.3 47.9 %all-to-all-done.1 = f32[8,17,32,128]{3,2,1,0:T(8,128)S(1)} async-done(((f32[8,17,32,128]{3,2,1,0:T(8,128)}), f32[8,17,32,128]{3,2,1,0:T(8,128)S(1)}, u32[]{:S(2)}, u32[]{:S(2)}) %all-to-all-start.1) | async-done | bytes 2228256 | tf_op jit(solution)/shard_map/all_to_all | solution.py:427
  198.3 0.0 copy-start
  198.3 1.3 copy-done
  199.6 12.6 %shard_map.250 = f32[4352,128]{1,0:T(8,128)} custom-call(s32[2]{0:T(128)} %pad_add_fusion.1.place, f32[4352,128]{1,0:T(8,128)} %bitcast.15, bf16[256,272]{1,0:T(8,128)(2,1)} %constant.50.clone.hx_hi, bf16[256,272]{1,0:T(8,128)(2,1)} %constant.51.clone.hx_lo, bf16[272,256]{1,0:T(8,128)(2,1)} %constant.52.clone.ix_hi, bf16[272,256]{1,0:T(8,128)(2,1)} %constant.53.clone.ix_lo), custom_call_target="tpu_custom_call" | custom-call | tf_op jit(solution)/shard_map/pallas_call | solution.py:324
  212.2 54.9 %all_to_all.21.data = f32[8,17,32,128]{3,2,1,0:T(8,128)} all-to-all(f32[8,17,32,128]{3,2,1,0:T(8,128)} %bitcast.16), channel_id=1, replica_groups=mesh['grp'=4,'dom'=8] {'dom'}, dimensions={0} | all-to-all | bytes 4456448 | tf_op jit(solution)/shard_map/all_to_all | solution.py:436
  267.1 5.3 %shard_map.251 = f32[4,17,72,128]{3,2,1,0:T(8,128)} custom-call(f32[8,17,32,128]{3,2,1,0:T(8,128)} %all_to_all.21.data, bf16[288,256]{1,0:T(8,128)(2,1)} %constant.54.clone.hy_hi, bf16[288,256]{1,0:T(8,128)(2,1)} %constant.55.clone.hy_lo), custom_call_target="tpu_custom_call" | custom-call | tf_op jit(solution)/shard_map/pallas_call | solution.py:324
  272.4 36.2 %all_to_all.22.data = f32[4,17,72,128]{3,2,1,0:T(8,128)} all-to-all(f32[4,17,72,128]{3,2,1,0:T(8,128)} %shard_map.251), channel_id=1, replica_groups=mesh['grp'=4,'dom'=8] {'grp'}, dimensions={0} | all-to-all | bytes 5013504 | tf_op jit(solution)/shard_map/all_to_all | solution.py:440
  308.6 9.2 %shard_map.252 = (f32[16,128]{1,0:T(8,128)}, f32[3,2048]{1,0:T(4,128)}) custom-call(s32[3,2048]{1,0:T(4,128)} %broadcast_add_fusion.local, f32[3,2048]{1,0:T(4,128)} %frac.3, f32[16,128]{1,0:T(8,128)} %get-tuple-element.7.charge, f32[16,128]{1,0:T(8,128)} %get-tuple-element.8.energy, f32[4,17,72,128]{3,2,1,0:T(8,128)} %all_to_all.22.data, ...), custom_call_target="tpu_custom_call" | custom-call | tf_op jit(solution)/shard_map/pallas_call | solution.py:324
  (4 shorter events, 0.1 us)
Async XLA Ops:
  2.1 13.7 %collective-permute-start = (f32[4,2048]{1,0:T(4,128)S(1)}, f32[4,2048]{1,0:T(4,128)S(1)}, u32[]{:S(2)}, u32[]{:S(2)}) collective-permute-start(f32[4,2048]{1,0:T(4,128)S(1)} %pad_maximum_fusion.1), channel_id=1, source_target_pairs={{0,1},{1,2},{2,3},{3,4},{4,5},{5,6},{6,7},{7,0},{8,9},{9,10},{10,1... | collective-permute-start | bytes 98312 | tf_op jit(solution)/shard_map/ppermute | solution.py:408
  3.4 12.4 %collective-permute-start.1 = (f32[4,2048]{1,0:T(4,128)S(1)}, f32[4,2048]{1,0:T(4,128)S(1)}, u32[]{:S(2)}, u32[]{:S(2)}) collective-permute-start(f32[4,2048]{1,0:T(4,128)S(1)} %pad_maximum_fusion.1), channel_id=1, source_target_pairs={{1,0},{2,1},{3,2},{4,3},{5,4},{6,5},{7,6},{0,7},{9,8},{10,9},{11,1... | collective-permute-start | bytes 98312 | tf_op jit(solution)/shard_map/ppermute | solution.py:409
  9.8 3.9 %copy-start.1 = (s32[4,2]{0,1:T(2,128)S(1)}, s32[4,2]{0,1:T(2,128)}, u32[]{:S(2)}) copy-start(s32[4,2]{0,1:T(2,128)} %param.27) | copy-start | bytes 100
  12.4 4.1 %copy-start.2 = (bf16[256]{0:T(256)(128)(2,1)S(1)}, bf16[256]{0:T(256)(128)(2,1)}, u32[]{:S(2)}) copy-start(bf16[256]{0:T(256)(128)(2,1)} %param.34) | copy-start | bytes 1540
  12.4 4.7 %copy-start.3 = (bf16[256]{0:T(256)(128)(2,1)S(1)}, bf16[256]{0:T(256)(128)(2,1)}, u32[]{:S(2)}) copy-start(bf16[256]{0:T(256)(128)(2,1)} %param.35) | copy-start | bytes 1540
  125.0 73.3 %all-to-all-start.1 = ((f32[8,17,32,128]{3,2,1,0:T(8,128)}), f32[8,17,32,128]{3,2,1,0:T(8,128)S(1)}, u32[]{:S(2)}, u32[]{:S(2)}) async-start(f32[8,17,32,128]{3,2,1,0:T(8,128)} %shard_map.249), calls=%async_computation.1 | async-start | bytes 4456448 | tf_op jit(solution)/shard_map/all_to_all | solution.py:427
  198.3 1.3 copy-start

commit v2 on v1

--- a/solution.py
+++ b/solution.py
@@ -54,16 +54,6 @@
     return dot(a[0], b[0]) + (dot(a[0], b[1]) + dot(a[1], b[0]))
 
 
-def rounded(x):
-    return lax.reduce_precision(x, exponent_bits=8, mantissa_bits=7)
-
-
-def split3_outer(x):
-    one = rounded(x)
-    two = rounded(x - one)
-    return one, two, rounded(x - one - two)
-
-
 def split3(x):
     one = x.astype(BF).astype(F32)
     two = (x - one).astype(BF).astype(F32)
@@ -72,78 +62,125 @@
 
 
 def pair_kernel(
-    slots, live, cols, ext, wcat, whid, wq, we, energy, charge, env_s, feat_s, kind_s, pq_s, pe_s, *, step
+    slots,
+    live,
+    left,
+    own,
+    right,
+    radial_w,
+    kind_i_w,
+    kind_j_w,
+    hidden_w,
+    charge_w,
+    energy_w,
+    energy,
+    charge,
+    ext,
+    wcat,
+    whid,
+    rank_s,
+    theta_s,
+    env_s,
+    kind_s,
+    *,
+    step,
 ):
     blocks = energy.shape[0]
+    atoms = own.shape[1]
     energy[...] = jnp.zeros_like(energy)
     charge[...] = jnp.zeros_like(charge)
+    ext[:, :atoms] = left[...]
+    ext[:, atoms : 2 * atoms] = own[...]
+    ext[:, 2 * atoms :] = right[...]
+    width = hidden_w.shape[0]
+    r1, r2, r3 = split3(radial_w[...])
+    table = jnp.concatenate(
+        [
+            *(r1, r2, r3, r1, r2, r1),
+            *split3(kind_j_w[...]),
+            *split3(kind_i_w[...]),
+            jnp.zeros((BLOCK - 12 * NBASIS, width), F32),
+        ],
+        axis=0,
+    )
+    wcat[...] = (0.5 * table).T.astype(BF)
+    whid[...] = (0.5 * hidden_w[...].astype(F32)).T.astype(BF)
+    wq = jnp.broadcast_to(charge_w[...].astype(F32), (16, width)).astype(BF)
+    we = jnp.broadcast_to(energy_w[...].astype(F32), (16, width)).astype(BF)
     half = 0.5 * G
     row8 = lax.broadcasted_iota(jnp.int32, (NSPEC, BLOCK), 0).astype(F32)
-    diag = lax.broadcasted_iota(jnp.int32, (BLOCK, BLOCK), 0) == lax.broadcasted_iota(
-        jnp.int32, (BLOCK, BLOCK), 1
-    )
+    sub = lax.broadcasted_iota(jnp.int32, (BLOCK, BLOCK), 0)
+    lane = lax.broadcasted_iota(jnp.int32, (BLOCK, BLOCK), 1)
+    earlier = (lane < sub).astype(F32).astype(BF)
+    spare = jnp.zeros((BLOCK - 12 * NBASIS, BLOCK), F32)
 
     def slot_body(slot, unused):
         bi = slots[slot, 0]
         bj = slots[slot, 1]
-        ci = cols[pl.ds(pl.multiple_of(bi * BLOCK, BLOCK), BLOCK), :]
+        ri = own[:, pl.ds(pl.multiple_of(bi * BLOCK, BLOCK), BLOCK)]
         rj = ext[:, pl.ds(pl.multiple_of(bj * BLOCK, BLOCK), BLOCK)]
         total = jnp.zeros((BLOCK, BLOCK), F32)
         for c in range(3):
-            sep = rj[c : c + 1, :] - ci[:, c : c + 1]
+            sep = jnp.broadcast_to(rj[c : c + 1, :], (BLOCK, BLOCK)).T - ri[c : c + 1, :]
             sep = jnp.where(sep > half, sep - G, jnp.where(sep < -half, sep + G, sep))
             total = total + sep * sep
         scaled = jnp.sqrt(total) / CUTOFF
         inside = 1.0 - scaled * scaled
         env = jnp.where(scaled < 1.0, inside * inside, 0.0)
-        env = jnp.where(diag & (bj == blocks + bi), 0.0, env)
+        env = jnp.where((sub == lane) & (bj == blocks + bi), 0.0, env)
+        used = (env > 0.0).astype(F32)
+        rank_s[...] = jnp.where(env > 0.0, dot_nn(earlier, used.astype(BF)), -1.0)
+        theta_s[...] = math.pi * jnp.minimum(scaled, 1.0)
         env_s[...] = env
-        kind_s[...] = jnp.broadcast_to(ci[:, 3:4], (BLOCK, BLOCK))
-        theta = math.pi * jnp.minimum(scaled, 1.0)
-        small = theta == 0.0
-        inv = 1.0 / jnp.where(small, 1.0, theta)
-        twice = 2.0 * jnp.cos(theta)
-        before = jnp.zeros_like(theta)
-        now = jnp.sin(theta)
-        for n in range(1, NBASIS + 1):
-            feat_s[pl.ds(n - 1, BLOCK, stride=NBASIS), :] = jnp.where(
-                small, 1.0, now * inv * (1.0 / n)
-            )
-            before, now = now, twice * now - before
-        kind_j = (row8 == rj[3:4, :]).astype(F32)
-
-        def rows_body(it, unused_rows):
-            i0 = it * step
+        kind_s[...] = jnp.broadcast_to(rj[3:4, :], (BLOCK, BLOCK)).T
+        most = jnp.max(jnp.sum(used, axis=0, keepdims=True)).astype(jnp.int32)
+        kind_i = (row8 == ri[3:4, :]).astype(F32)
+
+        def rows_body(it, sums):
+            energy_sum, charge_sum = sums
+            rank = rank_s[...]
             parts = []
+            envs = []
             for k in range(step):
-                i = i0 + k
-                rad = feat_s[pl.ds(pl.multiple_of(i * NBASIS, NBASIS), NBASIS), :]
+                pick = rank == (it * step + k).astype(F32)
+                theta = jnp.sum(jnp.where(pick, theta_s[...], 0.0), axis=0, keepdims=True)
+                kind = jnp.sum(jnp.where(pick, kind_s[...], 0.0), axis=0, keepdims=True)
+                envs.append(jnp.sum(jnp.where(pick, env_s[...], 0.0), axis=0, keepdims=True))
+                phase = theta * (row8 + 1.0)
+                small = phase == 0.0
+                rad = jnp.where(small, 1.0, jnp.sin(phase) / jnp.where(small, 1.0, phase))
                 one, two, three = split3(rad)
-                kind_i = (row8 == kind_s[pl.ds(i, 1), :]).astype(F32)
+                kind_j = (row8 == kind).astype(F32)
                 parts.append(
                     jnp.concatenate(
-                        [one, one, one, two, two, three, kind_j, kind_j, kind_j, kind_i, kind_i, kind_i],
+                        [
+                            *(one, one, one, two, two, three),
+                            *(kind_j, kind_j, kind_j, kind_i, kind_i, kind_i),
+                            spare,
+                        ],
                         axis=0,
                     ).astype(BF)
                 )
             feats = jnp.concatenate(parts, axis=1)
             h = dot_nn(wcat[...], feats)
             edge = (h + h * jnp.tanh(h)).astype(BF)
-            cp = dot_nn(wq[...], edge)
+            cp = dot_nn(wq, edge)
             g = dot_nn(whid[...], edge)
             latent = (g + g * jnp.tanh(g)).astype(BF)
-            ep = dot_nn(we[...], latent)
+            ep = dot_nn(we, latent)
             for k in range(step):
-                row = pl.ds(i0 + k, 1)
-                env_row = env_s[row, :]
-                pq_s[row, :] = env_row * cp[0:1, k * BLOCK : (k + 1) * BLOCK]
-                pe_s[row, :] = env_row * ep[0:1, k * BLOCK : (k + 1) * BLOCK]
-            return unused_rows
-
-        lax.fori_loop(0, BLOCK // step, rows_body, 0)
+                cut = slice(k * BLOCK, (k + 1) * BLOCK)
+                charge_sum = charge_sum + envs[k] * cp[0:1, cut]
+                energy_sum = energy_sum + envs[k] * ep[0:1, cut]
+            return energy_sum, charge_sum
+
+        zero = jnp.zeros((1, BLOCK), F32)
+        energy_sum, charge_sum = lax.fori_loop(
+            0, (most + step - 1) // step, rows_body, (zero, zero)
+        )
         where = pl.ds(bi, 1)
-        charge[where, :] = charge[where, :] + jnp.sum(pq_s[...].T, axis=0, keepdims=True)
-        energy[where, :] = energy[where, :] + jnp.sum(pe_s[...].T, axis=0, keepdims=True)
+        charge[where, :] = charge[where, :] + charge_sum
+        energy[where, :] = energy[where, :] + energy_sum
         return unused
 
     lax.fori_loop(0, live[0], slot_body, 0)
@@ -331,29 +368,36 @@
     )(*args)
 
 
-def pair_weights(species_embed, neighbour_embed, w_radial, w_hidden, w_charge, w_energy):
-    r1, r2, r3 = split3_outer(w_radial)
-    table = jnp.concatenate(
-        [r1, r2, r3, r1, r2, r1, *split3_outer(neighbour_embed), *split3_outer(species_embed)], axis=0
-    )
-    wcat = (0.5 * table).T.astype(BF)
-    whid = (0.5 * w_hidden.astype(F32)).T.astype(BF)
+def pair_call(
+    pair_blocks, counts, left, record, right, species_embed, neighbour_embed, w_radial, w_hidden, w_charge, w_energy
+):
+    blocks = record.shape[1] // BLOCK
     width = w_charge.shape[0]
-    wq = jnp.broadcast_to(w_charge[None, :], (16, width))
-    we = jnp.broadcast_to(w_energy[None, :], (16, width))
-    return wcat, whid, wq, we
-
-
-def pair_call(pair_blocks, counts, record, extended, weights, blocks):
-    cols = jnp.pad(record.T, ((0, 0), (0, 4)))
     shape = jax.ShapeDtypeStruct((blocks, BLOCK), F32)
     square = pltpu.VMEM((BLOCK, BLOCK), F32)
     return call(
         functools.partial(pair_kernel, step=4),
         [shape, shape],
-        [square, pltpu.VMEM((BLOCK * NBASIS, BLOCK), F32), square, square, square],
+        [
+            pltpu.VMEM((record.shape[0], 3 * record.shape[1]), F32),
+            pltpu.VMEM((width, BLOCK), BF),
+            pltpu.VMEM((width, width), BF),
+            *[square] * 4,
+        ],
         2,
-        (pair_blocks, counts, cols, extended, *weights),
+        (
+            pair_blocks,
+            counts,
+            left,
+            record,
+            right,
+            w_radial,
+            species_embed,
+            neighbour_embed,
+            w_hidden,
+            w_charge[None, :],
+            w_energy[None, :],
+        ),
     )
 
 
@@ -407,9 +451,19 @@
     record = jnp.concatenate([positions, species.astype(F32)[None, :]], axis=0)
     left = lax.ppermute(record, "dom", [(i, (i + 1) % doms) for i in range(doms)])
     right = lax.ppermute(record, "dom", [((i + 1) % doms, i) for i in range(doms)])
-    extended = jnp.concatenate([left, record, right], axis=1)
-    weights = pair_weights(species_embed, neighbour_embed, w_radial, w_hidden, w_charge, w_energy)
-    energies, charges = pair_call(pair_blocks, counts, record, extended, weights, blocks)
+    energies, charges = pair_call(
+        pair_blocks,
+        counts,
+        left,
+        record,
+        right,
+        species_embed,
+        neighbour_embed,
+        w_radial,
+        w_hidden,
+        w_charge,
+        w_energy,
+    )
 
     origin = jnp.stack([1 - slab * dom_id, 1 - quarter * grp_id, jnp.zeros_like(dom_id)])
     local = cell_index + origin[:, None]

time: 322 us -> 245 us (0.76)
  blocking collectives: 163 us -> 124 us
  Pallas kernels: 63 us -> 47 us
  starting transfers between devices: 26.3 us -> 10.6 us
  other arithmetic: 7.75 us -> 3.59 us
    all_to_all x2, blocking collectives: 108 us -> 69 us  [on_device(): spec = lax.all_to_all(spec, 'grp', 0, 0, tiled=True)]
    all_to_all x1, starting transfers between devices: 24.8 us -> 8.17 us  [on_device(): spec = lax.all_to_all(spec, 'dom', 0, 0, tiled=True)]
    pallas_call x6, Pallas kernels: 63 us -> 47 us  [call(): pl.pallas_call(body, out_shape=outs, in_specs=specs, out_specs=[VMEM_SPEC...]
  transfers between devices with their start and end apart: 3 -> 3, of which waited for: 1 -> 1; matrix products, arithmetic and copies ran while one was open for 4% -> 2% of each run, Pallas kernels for 0% -> 0%
where the time goes in v2:
time: 245 us; the launch traced here: 241 us
  blocking collectives  124 us (51%)
  waiting for transfers between devices  47.9 us (20%)
  Pallas kernels  47 us (19%)
  starting transfers between devices  10.6 us (4%)
  local copies, waits for them, and re-layouts  6.28 us (3%)
  other arithmetic  3.59 us (1%)
    all_to_all x2, blocking collectives, on_device(): spec = lax.all_to_all(spec, 'grp', 0, 0, tiled=True)  69 us
    all_to_all x1, blocking collectives, on_device(): lax.all_to_all(spec.reshape(doms, pairs, width_y, BLOCK), 'dom', 0, 0, ti...  54.9 us
    all_to_all x1, waiting for transfers between devices, on_device(): spec = lax.all_to_all(spec, 'dom', 0, 0, tiled=True)  47.9 us
    pallas_call x6, Pallas kernels, call(): pl.pallas_call(body, out_shape=outs, in_specs=specs, out_specs=[VMEM_SPEC...  47 us
    all_to_all x1, starting transfers between devices, on_device(): spec = lax.all_to_all(spec, 'dom', 0, 0, tiled=True)  8.17 us
  transfers between devices with their start and end apart: 3, of which 1 were waited for; matrix products, arithmetic and copies ran while one was open for 2% of the time, Pallas kernels for 0%

profile of v2, /device:TPU:13, one launch (start us, length us, event | category | flops | bytes accessed | tf_op | source)
XLA Modules:
  0.0 240.7 jit_solution(3894339030354428494)
XLA Ops:
  0.6 0.7 convert_element_type.7
  1.3 0.8 convert_add_fusion
  2.1 0.0 copy-start.1
  2.2 0.3 collective-permute-start.1
  2.4 2.1 collective-permute-start
  4.6 0.1 pad_add_fusion
  4.6 1.4 broadcast_add_fusion.local
  6.7 1.2 broadcast_in_dim.11.charge_w
  7.9 1.2 broadcast_in_dim.12.energy_w
  9.1 1.3 copy.27.slots
  10.5 0.0 collective-permute-done.1.right
  10.5 0.0 copy-start.2
  10.5 0.0 collective-permute-done.left
  10.5 0.0 copy-done.1
  10.5 0.6 copy-done.2
  11.1 0.0 copy-start.3
  11.1 0.6 copy-done.3
  11.7 5.2 %shard_map.247 = (f32[16,128]{1,0:T(8,128)}, f32[16,128]{1,0:T(8,128)}) custom-call(s32[4,2]{1,0:T(4,128)} %copy.27.slots, s32[1]{0:T(128)S(6)} %copy.28.live, f32[4,2048]{1,0:T(4,128)} %copy-done.3, f32[4,2048]{1,0:T(4,128)} %copy-done.1, f32[4,2048]{1,0:T(4,128)} %copy-done.2, f32[8,256]{1,0:T(8,128)} %radial_w.1, f32[8,256]{1,0:T(8,128)} %kind_i_w.1, ...), custom_call_target="tpu_custom_call" | custom-call | tf_op jit(solution)/shard_map/pallas_call | solution.py:361
  16.9 8.7 %shard_map.248 = f32[4,17,72,128]{3,2,1,0:T(8,128)} custom-call(s32[3,2048]{1,0:T(4,128)} %broadcast_add_fusion.local, f32[3,2048]{1,0:T(4,128)} %frac.3, f32[16,128]{1,0:T(8,128)} %get-tuple-element.7.charge, f32[32,64,256]{2,1,0:T(8,128)} %back.1, bf16[256,512]{1,0:T(8,128)(2,1)} %constant.40.clone.hz_hi, bf16[256,512]{1,0:T(8,128)(2,1)} %constant.41.clone.hz_lo), custom_call_target="tpu_custom_call" | custom-call | tf_op jit(solution)/shard_map/pallas_call | solution.py:361
  25.6 32.8 %all_to_all.20.data = f32[4,17,72,128]{3,2,1,0:T(8,128)} all-to-all(f32[4,17,72,128]{3,2,1,0:T(8,128)} %shard_map.248), channel_id=1, replica_groups=mesh['grp'=4,'dom'=8] {'grp'}, dimensions={0} | all-to-all | bytes 5013504 | tf_op jit(solution)/shard_map/all_to_all | solution.py:477
  58.4 5.9 %shard_map.249 = f32[8,17,32,128]{3,2,1,0:T(8,128)} custom-call(f32[4,17,72,128]{3,2,1,0:T(8,128)} %all_to_all.20.data, bf16[256,288]{1,0:T(8,128)(2,1)} %constant.42.clone.hy_hi, bf16[256,288]{1,0:T(8,128)(2,1)} %constant.43.clone.hy_lo), custom_call_target="tpu_custom_call" | custom-call | tf_op jit(solution)/shard_map/pallas_call | solution.py:361
  64.4 8.2 %all-to-all-start.1 = ((f32[8,17,32,128]{3,2,1,0:T(8,128)}), f32[8,17,32,128]{3,2,1,0:T(8,128)S(1)}, u32[]{:S(2)}, u32[]{:S(2)}) async-start(f32[8,17,32,128]{3,2,1,0:T(8,128)} %shard_map.249), calls=%async_computation.1 | async-start | bytes 4456448 | tf_op jit(solution)/shard_map/all_to_all | solution.py:481
  72.6 0.6 pad_add_fusion.1.place
  73.1 47.9 %all-to-all-done.1 = f32[8,17,32,128]{3,2,1,0:T(8,128)S(1)} async-done(((f32[8,17,32,128]{3,2,1,0:T(8,128)}), f32[8,17,32,128]{3,2,1,0:T(8,128)S(1)}, u32[]{:S(2)}, u32[]{:S(2)}) %all-to-all-start.1) | async-done | bytes 2228256 | tf_op jit(solution)/shard_map/all_to_all | solution.py:481
  121.1 0.0 copy-start
  121.1 1.3 copy-done
  122.4 12.6 %shard_map.250 = f32[4352,128]{1,0:T(8,128)} custom-call(s32[2]{0:T(128)} %pad_add_fusion.1.place, f32[4352,128]{1,0:T(8,128)} %bitcast.9, bf16[256,272]{1,0:T(8,128)(2,1)} %constant.44.clone.hx_hi, bf16[256,272]{1,0:T(8,128)(2,1)} %constant.45.clone.hx_lo, bf16[272,256]{1,0:T(8,128)(2,1)} %constant.46.clone.ix_hi, bf16[272,256]{1,0:T(8,128)(2,1)} %constant.47.clone.ix_lo), custom_call_target="tpu_custom_call" | custom-call | tf_op jit(solution)/shard_map/pallas_call | solution.py:361
  135.0 54.9 %all_to_all.21.data = f32[8,17,32,128]{3,2,1,0:T(8,128)} all-to-all(f32[8,17,32,128]{3,2,1,0:T(8,128)} %bitcast.10), channel_id=1, replica_groups=mesh['grp'=4,'dom'=8] {'dom'}, dimensions={0} | all-to-all | bytes 4456448 | tf_op jit(solution)/shard_map/all_to_all | solution.py:490
  189.9 5.3 %shard_map.251 = f32[4,17,72,128]{3,2,1,0:T(8,128)} custom-call(f32[8,17,32,128]{3,2,1,0:T(8,128)} %all_to_all.21.data, bf16[288,256]{1,0:T(8,128)(2,1)} %constant.48.clone.hy_hi, bf16[288,256]{1,0:T(8,128)(2,1)} %constant.49.clone.hy_lo), custom_call_target="tpu_custom_call" | custom-call | tf_op jit(solution)/shard_map/pallas_call | solution.py:361
  195.3 36.2 %all_to_all.22.data = f32[4,17,72,128]{3,2,1,0:T(8,128)} all-to-all(f32[4,17,72,128]{3,2,1,0:T(8,128)} %shard_map.251), channel_id=1, replica_groups=mesh['grp'=4,'dom'=8] {'grp'}, dimensions={0} | all-to-all | bytes 5013504 | tf_op jit(solution)/shard_map/all_to_all | solution.py:494
  231.4 9.2 %shard_map.252 = (f32[16,128]{1,0:T(8,128)}, f32[3,2048]{1,0:T(4,128)}) custom-call(s32[3,2048]{1,0:T(4,128)} %broadcast_add_fusion.local, f32[3,2048]{1,0:T(4,128)} %frac.3, f32[16,128]{1,0:T(8,128)} %get-tuple-element.7.charge, f32[16,128]{1,0:T(8,128)} %get-tuple-element.8.energy, f32[4,17,72,128]{3,2,1,0:T(8,128)} %all_to_all.22.data, ...), custom_call_target="tpu_custom_call" | custom-call | tf_op jit(solution)/shard_map/pallas_call | solution.py:361
  (1 shorter events, 0.0 us)
Async XLA Ops:
  2.1 8.3 %copy-start.1 = (f32[4,2048]{1,0:T(4,128)}, f32[4,2048]{1,0:T(4,128)S(1)}, u32[]{:S(2)}) copy-start(f32[4,2048]{1,0:T(4,128)S(1)} %pad_maximum_fusion.own) | copy-start | bytes 98308
  2.2 8.3 %collective-permute-start.1 = (f32[4,2048]{1,0:T(4,128)S(1)}, f32[4,2048]{1,0:T(4,128)S(1)}, u32[]{:S(2)}, u32[]{:S(2)}) collective-permute-start(f32[4,2048]{1,0:T(4,128)S(1)} %pad_maximum_fusion.own), channel_id=1, source_target_pairs={{1,0},{2,1},{3,2},{4,3},{5,4},{6,5},{7,6},{0,7},{9,8},{10,9},{11,1... | collective-permute-start | bytes 98312 | tf_op jit(solution)/shard_map/ppermute | solution.py:453
  2.4 8.0 %collective-permute-start = (f32[4,2048]{1,0:T(4,128)S(1)}, f32[4,2048]{1,0:T(4,128)S(1)}, u32[]{:S(2)}, u32[]{:S(2)}) collective-permute-start(f32[4,2048]{1,0:T(4,128)S(1)} %pad_maximum_fusion.own), channel_id=1, source_target_pairs={{0,1},{1,2},{2,3},{3,4},{4,5},{5,6},{6,7},{7,0},{8,9},{9,10},{10,1... | collective-permute-start | bytes 98312 | tf_op jit(solution)/shard_map/ppermute | solution.py:452
  10.5 0.6 copy-start.2
  11.1 0.6 copy-start.3
  64.4 56.7 %all-to-all-start.1 = ((f32[8,17,32,128]{3,2,1,0:T(8,128)}), f32[8,17,32,128]{3,2,1,0:T(8,128)S(1)}, u32[]{:S(2)}, u32[]{:S(2)}) async-start(f32[8,17,32,128]{3,2,1,0:T(8,128)} %shard_map.249), calls=%async_computation.1 | async-start | bytes 4456448 | tf_op jit(solution)/shard_map/all_to_all | solution.py:481
  121.1 1.3 copy-start

commit v3 on v2

--- a/solution.py
+++ b/solution.py
@@ -244,15 +244,91 @@
             out[s, q] = jnp.where(low_half, piece[:padded_y], piece[padded_y:])
 
 
-def y_kernel(data, hy_hi, hy_lo, out):
-    groups, pairs = data.shape[0], data.shape[1]
-    parts, rows = out.shape[0], out.shape[2]
+def hop_kernel(
+    data, hy_hi, hy_lo, out, land, ready, send1, recv1, send2, recv2, local1, local2, *, axis1, axis2, cuts
+):
+    n1, n2 = land.shape[0], out.shape[0]
+    rows = out.shape[2]
+    me1, me2 = lax.axis_index(axis1), lax.axis_index(axis2)
+    mesh_ids = pl.DeviceIdType.MESH
+    barrier = pltpu.get_barrier_semaphore()
+    for axis, me, count in ((axis1, me1, n1), (axis2, me2, n2)):
+        for k in range(1, count):
+            pl.semaphore_signal(
+                barrier, inc=1, device_id={axis: lax.rem(me + k, count)}, device_id_type=mesh_ids
+            )
+    pl.semaphore_wait(barrier, n1 + n2 - 2)
+
+    def send(src, dst, send_sem, recv_sem, axis, me, count, k, c, part):
+        peer = lax.rem(me + k, count)
+        copy = pltpu.make_async_remote_copy(
+            src_ref=src.at[peer, part],
+            dst_ref=dst.at[me, part],
+            send_sem=send_sem.at[c, k - 1],
+            recv_sem=recv_sem.at[c, k - 1],
+            device_id={axis: peer},
+            device_id_type=mesh_ids,
+        )
+        copy.start()
+        return copy
+
+    first = []
+    for c, (lo, hi) in enumerate(cuts):
+        part = pl.ds(lo, hi - lo)
+        mine = pltpu.make_async_copy(data.at[me1, part], land.at[me1, part], local1.at[c])
+        mine.start()
+        first.append(
+            (mine, [send(data, land, send1, recv1, axis1, me1, n1, k, c, part) for k in range(1, n1)])
+        )
     table = (hy_hi[...], hy_lo[...])
-    for q in range(pairs):
-        column = jnp.concatenate([data[g, q] for g in range(groups)], axis=0)
-        result = dot3(dot_nn, table, split2(column))
-        for d in range(parts):
-            out[d, q] = result[d * rows : (d + 1) * rows]
+    second = []
+    for c, (lo, hi) in enumerate(cuts):
+        part = pl.ds(lo, hi - lo)
+        mine, copies = first[c]
+        mine.wait()
+        for copy in copies:
+            copy.wait_recv()
+        for q in range(lo, hi):
+            column = jnp.concatenate([land[g, q] for g in range(n1)], axis=0)
+            result = dot3(dot_nn, table, split2(column))
+            for d in range(n2):
+                ready[d, q] = result[d * rows : (d + 1) * rows]
+        own = pltpu.make_async_copy(ready.at[me2, part], out.at[me2, part], local2.at[c])
+        own.start()
+        second.append(
+            (own, [send(ready, out, send2, recv2, axis2, me2, n2, k, c, part) for k in range(1, n2)])
+        )
+    for mine, copies in first:
+        for copy in copies:
+            copy.wait_send()
+    for own, copies in second:
+        own.wait()
+        for copy in copies:
+            copy.wait()
+
+
+def hop_call(data, table, out_shape, axis1, axis2, collective):
+    n1, pairs = data.shape[0], data.shape[1]
+    n2 = out_shape[0]
+    chunks = min(4, pairs)
+    ends = [round(pairs * c / chunks) for c in range(chunks + 1)]
+    dma = pltpu.SemaphoreType.DMA
+    return pl.pallas_call(
+        functools.partial(hop_kernel, axis1=axis1, axis2=axis2, cuts=tuple(zip(ends[:-1], ends[1:]))),
+        out_shape=jax.ShapeDtypeStruct(out_shape, F32),
+        in_specs=[VMEM_SPEC] * 3,
+        out_specs=VMEM_SPEC,
+        scratch_shapes=[
+            pltpu.VMEM(data.shape, F32),
+            pltpu.VMEM(out_shape, F32),
+            *[dma((chunks, n1 - 1))] * 2,
+            *[dma((chunks, n2 - 1))] * 2,
+            *[dma((chunks,))] * 2,
+        ],
+        compiler_params=pltpu.CompilerParams(
+            vmem_limit_bytes=VMEM_BYTES, collective_id=collective, has_side_effects=True
+        ),
+    )(data, *table)
 
 
 def x_kernel(place, data, hx_hi, hx_lo, ix_hi, ix_lo, out, *, width_y):
@@ -474,11 +550,7 @@
         0,
         (local, offsets, charges, background, *hz_dup),
     )
-    spec = lax.all_to_all(spec, "grp", 0, 0, tiled=True)
-    spec = call(
-        y_kernel, jax.ShapeDtypeStruct((doms, pairs, width_y, BLOCK), F32), [], 0, (spec, *hy)
-    )
-    spec = lax.all_to_all(spec, "dom", 0, 0, tiled=True)
+    spec = hop_call(spec, hy, (doms, pairs, width_y, BLOCK), "grp", "dom", 0)
     place = jnp.stack([grp_id, dom_id]).astype(jnp.int32)
     spec = call(
         functools.partial(x_kernel, width_y=width_y),
@@ -487,11 +559,8 @@
         1,
         (place, spec.reshape(doms * pairs * width_y, BLOCK), *hx, *hx_inv),
     )
-    spec = lax.all_to_all(spec.reshape(doms, pairs, width_y, BLOCK), "dom", 0, 0, tiled=True)
-    spec = call(
-        y_kernel, jax.ShapeDtypeStruct((groups, pairs, padded_y, BLOCK), F32), [], 0, (spec, *hy_inv)
-    )
-    spec = lax.all_to_all(spec, "grp", 0, 0, tiled=True)
+    spec = spec.reshape(doms, pairs, width_y, BLOCK)
+    spec = hop_call(spec, hy_inv, (groups, pairs, padded_y, BLOCK), "dom", "grp", 1)
     site, field = call(
         sample_kernel,
         [jax.ShapeDtypeStruct((blocks, BLOCK), F32), jax.ShapeDtypeStruct((3, atoms), F32)],

time: 245 us -> 181 us (0.74); the launches traced: 241 us -> 180 us
  blocking collectives: 124 us -> 0 us
  Pallas kernels: 47 us -> 168 us
  waiting for transfers between devices: 47.9 us -> 0.01 us
  starting transfers between devices: 10.6 us -> 2.42 us
    pallas_call x0 -> x2, Pallas kernels: none -> 134 us  [hop_call(): pl.pallas_call(functools.partial(hop_kernel, axis1=axis1, axis2=axis2, cu...]
    all_to_all x3 -> x0, blocking collectives: 124 us -> none  [the longest x2 69 us: on_device(): spec = lax.all_to_all(spec, 'grp', 0, 0, tiled=True)]
    all_to_all x1 -> x0, waiting for transfers between devices: 47.9 us -> none  [on_device(): spec = lax.all_to_all(spec, 'dom', 0, 0, tiled=True)]
    pallas_call x6 -> x4, Pallas kernels: 47 us -> 34 us  [call(): pl.pallas_call(body, out_shape=outs, in_specs=specs, out_specs=[VMEM_SPEC...]
    all_to_all x1 -> x0, starting transfers between devices: 8.17 us -> none  [on_device(): spec = lax.all_to_all(spec, 'dom', 0, 0, tiled=True)]
  transfers between devices with their start and end apart: 3 -> 2, of which waited for: 1 -> 0; matrix products, arithmetic and copies ran while one was open for 2% -> 3% of each run, Pallas kernels for 0% -> 0%
where the time goes in v3:
time: 181 us; the launch traced here: 180 us
  Pallas kernels  168 us (93%)
  local copies, waits for them, and re-layouts  4.98 us (3%)
  other arithmetic  3.66 us (2%)
  starting transfers between devices  2.42 us (1%)
    pallas_call x2, Pallas kernels, hop_call(): pl.pallas_call(functools.partial(hop_kernel, axis1=axis1, axis2=axis2, cu...  134 us
    pallas_call x4, Pallas kernels, call(): pl.pallas_call(body, out_shape=outs, in_specs=specs, out_specs=[VMEM_SPEC...  34 us
  transfers between devices with their start and end apart: 2, of which 0 were waited for; matrix products, arithmetic and copies ran while one was open for 3% of the time, Pallas kernels for 0%

profile of v3, /device:TPU:13, one launch (start us, length us, event | category | flops | bytes accessed | tf_op | source)
XLA Modules:
  0.0 180.1 jit_solution(2769084469448536470)
XLA Ops:
  0.6 0.7 convert_element_type.7
  1.3 0.8 convert_add_fusion
  2.1 0.0 copy-start
  2.2 0.3 collective-permute-start.1
  2.4 2.1 %collective-permute-start = (f32[4,2048]{1,0:T(4,128)S(1)}, f32[4,2048]{1,0:T(4,128)S(1)}, u32[]{:S(2)}, u32[]{:S(2)}) collective-permute-start(f32[4,2048]{1,0:T(4,128)S(1)} %pad_maximum_fusion.own), channel_id=1, source_target_pairs={{0,1},{1,2},{2,3},{3,4},{4,5},{5,6},{6,7},{7,0},{8,9},{9,10},{10,1... | collective-permute-start | bytes 98312 | tf_op jit(solution)/shard_map/ppermute | solution.py:528
  4.6 0.1 pad_add_fusion
  4.6 1.4 broadcast_add_fusion.local
  6.1 0.6 pad_add_fusion.1.place
  7.4 1.2 broadcast_in_dim.11.charge_w
  8.6 1.2 broadcast_in_dim.12.energy_w
  9.8 1.3 copy.27.slots
  11.1 0.0 collective-permute-done.1.right
  11.2 0.0 copy-start.1
  11.2 0.0 collective-permute-done.left
  11.2 0.0 copy-done
  11.2 0.6 copy-done.1
  11.8 0.0 copy-start.2
  11.8 0.6 copy-done.2
  12.4 3.5 %shard_map.247 = (f32[16,128]{1,0:T(8,128)}, f32[16,128]{1,0:T(8,128)}) custom-call(s32[4,2]{1,0:T(4,128)} %copy.27.slots, s32[1]{0:T(128)S(6)} %copy.28.live, f32[4,2048]{1,0:T(4,128)} %copy-done.2, f32[4,2048]{1,0:T(4,128)} %copy-done, f32[4,2048]{1,0:T(4,128)} %copy-done.1, f32[8,256]{1,0:T(8,128)} %radial_w.1, f32[8,256]{1,0:T(8,128)} %kind_i_w.1, ...), custom_call_target="tpu_custom_call" | custom-call | tf_op jit(solution)/shard_map/pallas_call | solution.py:437
  15.9 8.6 %shard_map.248.data = f32[4,17,72,128]{3,2,1,0:T(8,128)} custom-call(s32[3,2048]{1,0:T(4,128)} %broadcast_add_fusion.local, f32[3,2048]{1,0:T(4,128)} %frac.3, f32[16,128]{1,0:T(8,128)} %get-tuple-element.7.charge, f32[32,64,256]{2,1,0:T(8,128)} %back.1, bf16[256,512]{1,0:T(8,128)(2,1)} %constant.40.clone.hz_hi, bf16[256,512]{1,0:T(8,128)(2,1)} %constant.41.clone.hz_lo), custom_call_target="tpu_custom_call" | custom-call | tf_op jit(solution)/shard_map/pallas_call | solution.py:437
  24.6 66.5 %shard_map.249 = f32[8,17,32,128]{3,2,1,0:T(8,128)} custom-call(f32[4,17,72,128]{3,2,1,0:T(8,128)} %shard_map.248.data, bf16[256,288]{1,0:T(8,128)(2,1)} %constant.42.clone.hy_hi, bf16[256,288]{1,0:T(8,128)(2,1)} %constant.43.clone.hy_lo), custom_call_target="tpu_custom_call" | custom-call | tf_op jit(solution)/shard_map/pallas_call | solution.py:316
  91.1 12.6 %shard_map.250 = f32[4352,128]{1,0:T(8,128)} custom-call(s32[2]{0:T(128)} %pad_add_fusion.1.place, f32[4352,128]{1,0:T(8,128)} %bitcast.9, bf16[256,272]{1,0:T(8,128)(2,1)} %constant.44.clone.hx_hi, bf16[256,272]{1,0:T(8,128)(2,1)} %constant.45.clone.hx_lo, bf16[272,256]{1,0:T(8,128)(2,1)} %constant.46.clone.ix_hi, bf16[272,256]{1,0:T(8,128)(2,1)} %constant.47.clone.ix_lo), custom_call_target="tpu_custom_call" | custom-call | tf_op jit(solution)/shard_map/pallas_call | solution.py:437
  103.7 67.1 %shard_map.251.data = f32[4,17,72,128]{3,2,1,0:T(8,128)} custom-call(f32[8,17,32,128]{3,2,1,0:T(8,128)} %bitcast.10, bf16[288,256]{1,0:T(8,128)(2,1)} %constant.48.clone.hy_hi, bf16[288,256]{1,0:T(8,128)(2,1)} %constant.49.clone.hy_lo), custom_call_target="tpu_custom_call" | custom-call | tf_op jit(solution)/shard_map/pallas_call | solution.py:316
  170.8 9.2 %shard_map.252 = (f32[16,128]{1,0:T(8,128)}, f32[3,2048]{1,0:T(4,128)}) custom-call(s32[3,2048]{1,0:T(4,128)} %broadcast_add_fusion.local, f32[3,2048]{1,0:T(4,128)} %frac.3, f32[16,128]{1,0:T(8,128)} %get-tuple-element.7.charge, f32[16,128]{1,0:T(8,128)} %get-tuple-element.8.energy, f32[4,17,72,128]{3,2,1,0:T(8,128)} %shard_map.251.data, ...), custom_call_target="tpu_custom_call" | custom-call | tf_op jit(solution)/shard_map/pallas_call | solution.py:437
  (1 shorter events, 0.0 us)
Async XLA Ops:
  2.1 9.0 %copy-start = (f32[4,2048]{1,0:T(4,128)}, f32[4,2048]{1,0:T(4,128)S(1)}, u32[]{:S(2)}) copy-start(f32[4,2048]{1,0:T(4,128)S(1)} %pad_maximum_fusion.own) | copy-start | bytes 98308
  2.2 9.0 %collective-permute-start.1 = (f32[4,2048]{1,0:T(4,128)S(1)}, f32[4,2048]{1,0:T(4,128)S(1)}, u32[]{:S(2)}, u32[]{:S(2)}) collective-permute-start(f32[4,2048]{1,0:T(4,128)S(1)} %pad_maximum_fusion.own), channel_id=1, source_target_pairs={{1,0},{2,1},{3,2},{4,3},{5,4},{6,5},{7,6},{0,7},{9,8},{10,9},{11,1... | collective-permute-start | bytes 98312 | tf_op jit(solution)/shard_map/ppermute | solution.py:529
  2.4 8.7 %collective-permute-start = (f32[4,2048]{1,0:T(4,128)S(1)}, f32[4,2048]{1,0:T(4,128)S(1)}, u32[]{:S(2)}, u32[]{:S(2)}) collective-permute-start(f32[4,2048]{1,0:T(4,128)S(1)} %pad_maximum_fusion.own), channel_id=1, source_target_pairs={{0,1},{1,2},{2,3},{3,4},{4,5},{5,6},{6,7},{7,0},{8,9},{9,10},{10,1... | collective-permute-start | bytes 98312 | tf_op jit(solution)/shard_map/ppermute | solution.py:528
  11.2 0.6 copy-start.1
  11.8 0.6 copy-start.2
